TPU v7x, 32 devices: a whole 2x2x4 slice. The times are simulated.
32 devices in a mesh: dp: 32 (over z, y, x, core).
Axes of the slice: x: 2, y: 2, z: 4, core: 2. Of those that a mesh axis runs over, the one named last changes fastest.
Arguments:
- events: bfloat16 [32768, 512], P('dp'), may hold values from -6 to 6
- home_slot: int32 [32768], P('dp'), may hold values from 0 to 1024, as said below
- dest_slot: int32 [32768], P('dp'), may hold values from 0 to 1024, as said below
- seq_lens: int32 [64], P('dp'), may hold values from 0 to 1024, as said below
- weights: bfloat16 [512, 2560], replicated, may hold values from -0.25 to 0.25
- out_grad: bfloat16 [32768, 512], P('dp'), may hold values from -6 to 6
- momentum_in: float32 [512, 2048], P('dp'), may hold values from -3 to 3
- momentum_out: float32 [512, 512], P('dp'), may hold values from -3 to 3
Outputs:
- event_grad: bfloat16 [32768, 512], P('dp')
- new_momentum_in: float32 [512, 2048], P('dp')
- new_momentum_out: float32 [512, 512], P('dp')
Inputs may be any that keep to these rules, and one draw needn't show every extreme that they name: `seq_lens`: each device's 2 entries are the lengths of the sequences placed on it, in order, then zeros; the sequences' blocks, ceil(length / 512) each, add up to at most 2. `dest_slot`: for each row of a device's blocks: 1024 if the row lies in no sequence, else s * 32 + k, where s is the device that holds the row's event at home and k its slot among the rows that s sends to this device; no value below 1024 repeats on a device. `home_slot`: for each home row: 1024 if no sequence uses it, else t * 32 + k, where t is the device that takes the row and k its slot as in dest_slot; no value below 1024 repeats on a device, and the two arrays name the same rows. A device sends at most 32 rows to one device, and in every draw some device receives 32 rows from every device.
All inputs are finite; a program needn't handle non-finite values.
Results may differ from a plain program's by a relative error of at most 0.0085.
Values may be sent and summed in bfloat16 or wider, within the bound.
A program may use at most 128 MiB of HBM per device.

v0:
```python
import jax
import jax.numpy as jnp
from jax import lax
from jax.sharding import PartitionSpec as P

HEADS = 8
BLK = 512


NORM_EPS = 1e-05
DECAY = 0.9


def row_owner(lengths, row_count):
    blocks = (lengths + BLK - 1) // BLK
    starts = (jnp.cumsum(blocks) - blocks) * BLK
    places = jnp.arange(row_count, dtype=jnp.int32)
    inside = (places[:, None] >= starts[None, :]) & (
        places[:, None] < starts[None, :] + lengths[None, :]
    )
    labels = jnp.arange(lengths.shape[0], dtype=jnp.int32) + 1
    return jnp.sum(jnp.where(inside, labels[None, :], 0), axis=1) - 1


def attend_pair(queries, key_rows, value_rows, query_owner, key_owner, query_place, key_place):
    factor = queries.shape[2] ** (-0.5)
    scores = (
        jnp.einsum("qhe,khe->hqk", queries, key_rows, preferred_element_type=jnp.float32) * factor
    )
    allowed = (
        (query_owner[:, None] == key_owner[None, :])
        & (query_owner[:, None] >= 0)
        & (key_place[None, :] <= query_place[:, None])
    )
    weights = jnp.where(allowed[None], jax.nn.silu(scores), 0.0).astype(jnp.bfloat16)
    return jnp.einsum("hqk,khe->qhe", weights, value_rows, preferred_element_type=jnp.float32)


def attend_block(query_set, key_set, value_set, owners, places, qblock):
    low_row = qblock * BLK
    high_row = low_row + BLK
    return jax.checkpoint(attend_pair)(
        query_set[low_row:high_row],
        key_set[:high_row],
        value_set[:high_row],
        owners[low_row:high_row],
        owners[:high_row],
        places[low_row:high_row],
        places[:high_row],
    )


def mixing(hidden, owners):
    activated = jax.nn.silu(hidden)
    model_width = hidden.shape[1] // 4
    row_count = hidden.shape[0]
    head_size = model_width // HEADS
    gate_part = activated[:, :model_width]
    value_set = (
        activated[:, model_width : 2 * model_width]
        .astype(jnp.bfloat16)
        .reshape(row_count, HEADS, head_size)
    )
    query_set = (
        activated[:, 2 * model_width : 3 * model_width]
        .astype(jnp.bfloat16)
        .reshape(row_count, HEADS, head_size)
    )
    key_set = (
        activated[:, 3 * model_width :].astype(jnp.bfloat16).reshape(row_count, HEADS, head_size)
    )
    places = jnp.arange(row_count, dtype=jnp.int32)
    pieces = [
        attend_block(query_set, key_set, value_set, owners, places, qblock)
        for qblock in range(row_count // BLK)
    ]
    attended = jnp.concatenate(pieces, axis=0).reshape(row_count, model_width)
    centre = jnp.mean(attended, axis=1, keepdims=True)
    centred = attended - centre
    spread = jnp.mean(centred * centred, axis=1, keepdims=True)
    return centred * lax.rsqrt(spread + NORM_EPS) * gate_part


def shards(events, home_slot, dest_slot, seq_lens, weights, out_grad, momentum_in, momentum_out):
    row_count, model_width = events.shape
    zero_row = jnp.zeros((1, model_width), jnp.bfloat16)
    outbox = (
        jnp.zeros((row_count + 1, model_width), jnp.bfloat16).at[home_slot].set(events)[:row_count]
    )
    inbox = lax.all_to_all(outbox, "dp", split_axis=0, concat_axis=0, tiled=True)
    tokens = jnp.concatenate([inbox, zero_row], axis=0)[dest_slot]
    owners = row_owner(seq_lens, row_count)
    w_in = weights[:, : 4 * model_width]
    w_out = weights[:, 4 * model_width :]
    hidden = jnp.dot(tokens, w_in, preferred_element_type=jnp.float32)
    mixed_out, pullback = jax.vjp(lambda hidden_in: mixing(hidden_in, owners), hidden)
    mixed_low = mixed_out.astype(jnp.bfloat16)
    out_term = lax.dot_general(
        mixed_low, out_grad, (((0,), (0,)), ((), ())), preferred_element_type=jnp.float32
    )
    grad_scale = (lax.axis_size("dp") * row_count) ** (-0.5)
    mixed_grad = lax.dot_general(
        out_grad, w_out, (((1,), (1,)), ((), ())), preferred_element_type=jnp.float32
    )
    hidden_grad = pullback(mixed_grad)[0].astype(jnp.bfloat16)
    in_term = lax.dot_general(
        tokens, hidden_grad, (((0,), (0,)), ((), ())), preferred_element_type=jnp.float32
    )
    token_grad = (
        out_grad.astype(jnp.float32)
        + lax.dot_general(
            hidden_grad, w_in, (((1,), (1,)), ((), ())), preferred_element_type=jnp.float32
        )
    ).astype(jnp.bfloat16)
    sendback = (
        jnp.zeros((row_count + 1, model_width), jnp.bfloat16)
        .at[dest_slot]
        .set(token_grad)[:row_count]
    )
    returned = lax.all_to_all(sendback, "dp", split_axis=0, concat_axis=0, tiled=True)
    event_grad = jnp.concatenate([returned, zero_row], axis=0)[home_slot]
    in_sum, out_sum = (
        lax.psum_scatter(in_term, "dp", scatter_dimension=0, tiled=True),
        lax.psum_scatter(out_term, "dp", scatter_dimension=0, tiled=True),
    )
    return (
        event_grad,
        DECAY * momentum_in + grad_scale * in_sum,
        DECAY * momentum_out + grad_scale * out_sum,
    )


def solution(mesh):
    in_specs = (
        P("dp", None),
        P("dp"),
        P("dp"),
        P("dp"),
        P(),
        P("dp", None),
        P("dp", None),
        P("dp", None),
    )
    out_specs = (P("dp", None), P("dp", None), P("dp", None))
    return jax.shard_map(shards, mesh=mesh, in_specs=in_specs, out_specs=out_specs, check_vma=False)
```

profile of v0, /device:TPU:0, one launch (start us, length us, event | category | flops | bytes accessed | tf_op | source)
XLA Modules:
  0.0 407.6 jit_solution(16068027650786576429)
XLA Ops:
  8.4 5.8 %scatter_custom_fusion = bf16[1025,512]{1,0:T(8,128)(2,1)S(1)} fusion(s32[1024]{0:T(1024)S(1)} %get-tuple-element.53, bf16[1024,512]{1,0:T(8,128)(2,1)} %param.8, bf16[]{:T(256)} %constant.29.clone.1), kind=kCustom, calls=%fused_computation.73 | custom fusion | bytes 1050112 | tf_op jit(solution)/shard_map/scatter | solution.py:88
  15.3 7.3 %all-to-all-start = ((bf16[32,32,512]{2,1,0:T(8,128)(2,1)}), bf16[32,32,512]{2,1,0:T(8,128)(2,1)S(1)}, u32[]{:S(2)}, u32[]{:S(2)}) async-start(bf16[32,32,512]{2,1,0:T(8,128)(2,1)} %bitcast), calls=%async_computation | async-start | bytes 2097152 | tf_op jit(solution)/shard_map/all_to_all | solution.py:90
  27.4 21.4 %all-to-all-done = bf16[32,32,512]{2,1,0:T(8,128)(2,1)S(1)} async-done(((bf16[32,32,512]{2,1,0:T(8,128)(2,1)}), bf16[32,32,512]{2,1,0:T(8,128)(2,1)S(1)}, u32[]{:S(2)}, u32[]{:S(2)}) %all-to-all-start) | async-done | bytes 1048608 | tf_op jit(solution)/shard_map/all_to_all | solution.py:90
  48.9 4.0 gather_fusion
  52.9 9.3 %fusion.67 = (bf16[1024,2048]{1,0:T(8,128)(2,1)S(1)}, f32[1024,2048]{1,0:T(8,128)}, f32[1024,2048]{1,0:T(8,128)}) fusion(bf16[1024,512]{1,0:T(8,128)(2,1)S(1)} %gather_fusion, bf16[512,2560]{1,0:T(8,128)(2,1)} %param.12), kind=kOutput, calls=%fused_computation.117 | convolution fusion | flops 2157969408 | bytes 24117248 | tf_op jit(solution)/shard_map/dot_general | solution.py:95
  66.8 2.3 copy.53
  69.3 2.9 copy.51
  72.2 5.7 %fusion.26 = f32[512,8,64]{0,2,1:T(8,128)} fusion(bf16[512,8,64]{0,2,1:T(8,128)(2,1)} %bitcast.102, pred[512,512]{1,0:T(8,128)(4,1)S(1)} %compare_and_fusion.2, bf16[512,8,64]{0,2,1:T(8,128)(2,1)S(1)} %bitcast.91, bf16[512,8,64]{0,2,1:T(8,128)(2,1)S(1)} %bitcast.88), kind=kOutput, calls=%fused_computation.48 | convolution fusion | flops 551550976 | bytes 2883584 | tf_op jit(solution)/shard_map/jvp(hqk,khe->qhe)/dot_general | solution.py:36
  78.0 9.6 %fusion.25 = f32[512,8,64]{0,2,1:T(8,128)} fusion(bf16[1024,8,64]{0,2,1:T(8,128)(2,1)} %bitcast.99, bf16[512,8,64]{0,2,1:T(8,128)(2,1)S(1)} %bitcast.85, bf16[1024,8,64]{0,2,1:T(8,128)(2,1)S(1)} %bitcast.82, pred[512,1024]{1,0:T(8,128)(4,1)S(1)} %copy-done.15), kind=kOutput, calls=%fused_computation.47 | convolution fusion | flops 1103101952 | bytes 4194304 | tf_op jit(solution)/shard_map/jvp(hqk,khe->qhe)/dot_general | solution.py:36
  88.9 2.9 multiply_reduce_fusion.1
  93.9 4.3 %multiply_reduce_fusion = (f32[1024]{0:T(1024)S(1)}, f32[1024,512]{1,0:T(8,128)}) fusion(f32[1024,512]{1,0:T(8,128)S(1)} %copy.56, f32[1024]{0:T(1024)S(1)} %broadcast_multiply_fusion, f32[1024,2048]{1,0:T(8,128)} %get-tuple-element.40, bf16[1024,512]{1,0:T(8,128)(2,1)} %param.13, bf16[512,2560]{1,0:T(8,128)(2,1)} %param.12), kind=kOutput, calls=%fused_computation.33 | convolution fusion | flops 538967040 | bytes 7872512 | tf_op jit(solution)/shard_map/dot_general | solution.py:102
  98.2 3.7 fusion.35
  101.9 3.7 fusion.64
  106.1 2.5 fusion.74
  108.9 3.4 fusion.32
  112.3 4.7 %fusion.5 = bf16[8,512,512]{2,1,0:T(8,128)(2,1)S(1)} fusion(f32[8,512,512]{2,1,0:T(8,128)S(1)} %fusion.74, pred[512,512]{1,0:T(8,128)(4,1)S(1)} %compare_and_fusion.1, bf16[512,8,64]{0,2,1:T(8,128)(2,1)S(1)} %bitcast.103, bf16[512,8,64]{0,2,1:T(8,128)(2,1)S(1)} %bitcast.107), kind=kOutput, calls=%fused_computation.15 | convolution fusion | flops 297795584 | bytes 13893632 | tf_op jit(solution)/shard_map/transpose(jvp(jvp()))/checkpoint/hqk,khe->qhe/dot_general | solution.py:36
  122.1 3.5 fusion.73
  127.0 6.5 %fusion.30 = bf16[1024,8,64]{0,2,1:T(8,128)(2,1)} fusion(f32[8,512,1024]{2,1,0:T(8,128)S(1)} %fusion.73, pred[512,1024]{1,0:T(8,128)(4,1)S(1)} %compare_and_fusion, bf16[512,8,64]{0,2,1:T(8,128)(2,1)S(1)} %bitcast.105, bf16[512,8,64]{0,2,1:T(8,128)(2,1)S(1)} %copy-done.22), kind=kOutput, calls=%fused_computation.55 | convolution fusion | flops 568328192 | bytes 19398656 | tf_op jit(solution)/shard_map/transpose(jvp(jvp()))/checkpoint/hqk,khe->qhe/dot_general | solution.py:36
  133.5 12.4 %fusion.2 = bf16[8,512,1024]{2,1,0:T(8,128)(2,1)} fusion(f32[8,512,1024]{2,1,0:T(8,128)S(1)} %fusion.73, pred[512,1024]{1,0:T(8,128)(4,1)} %copy-done.16, bf16[1024,8,64]{0,2,1:T(8,128)(2,1)} %bitcast.100, bf16[512,8,64]{0,2,1:T(8,128)(2,1)} %bitcast.104), kind=kOutput, calls=%fused_computation.7 | convolution fusion | flops 595591168 | bytes 27262976 | tf_op jit(solution)/shard_map/transpose(jvp(jvp()))/checkpoint/hqk,khe->qhe/dot_general | solution.py:36
  145.9 7.0 %fusion.31 = bf16[512,8,64]{0,2,1:T(8,128)(2,1)} fusion(bf16[8,512,1024]{2,1,0:T(8,128)(2,1)} %fusion.2, bf16[1024,8,64]{0,2,1:T(8,128)(2,1)S(1)} %bitcast.84), kind=kOutput, calls=%fused_computation.56 | convolution fusion | flops 536870912 | bytes 9961472 | tf_op jit(solution)/shard_map/transpose(jvp(jvp()))/checkpoint/qhe,khe->hqk/dot_general | solution.py:28
  153.0 2.5 fusion.29
  157.0 2.3 pad_add_fusion
  159.3 2.3 copy.60
  161.6 2.3 copy.61
  163.9 6.6 %fusion.8 = bf16[1024,2048]{1,0:T(8,128)(2,1)S(1)} fusion(f32[1024,2048]{1,0:T(8,128)} %get-tuple-element.62, f32[1024,512]{1,0:T(8,128)S(1)} %copy-done.1, bf16[1024,512]{1,0:T(8,128)(2,1)} %copy.61, bf16[1024,512]{1,0:T(8,128)(2,1)} %copy.60, bf16[1024,512]{1,0:T(8,128)(2,1)S(1)} %copy.59), kind=kLoop, calls=%fused_computation.18 | loop fusion | flops 33554432 | bytes 17825792 | tf_op jit(solution)/shard_map/convert_element_type | solution.py:105
  172.5 4.3 %fusion.75 = f32[512,2048]{1,0:T(8,128)} fusion(bf16[1024,512]{1,0:T(8,128)(2,1)S(1)} %copy-done.6, bf16[1024,2048]{1,0:T(8,128)(2,1)S(1)} %fusion.8), kind=kOutput, calls=%fused_computation.124 | convolution fusion | flops 2147483648 | bytes 9437184 | tf_op jit(solution)/shard_map/dot_general | solution.py:106
  176.9 5.2 %add_convert_fusion = bf16[1024,512]{1,0:T(8,128)(2,1)S(1)} fusion(bf16[1024,512]{1,0:T(8,128)(2,1)S(1)} %copy-done.12, bf16[1024,2048]{1,0:T(8,128)(2,1)} %copy-done, bf16[512,2560]{1,0:T(8,128)(2,1)} %param.12), kind=kOutput, calls=%fused_computation.32 | convolution fusion | flops 2149056512 | bytes 8388608 | tf_op jit(solution)/shard_map/dot_general | solution.py:111
  182.1 5.5 %scatter_custom_fusion.1 = bf16[1025,512]{1,0:T(8,128)(2,1)S(1)} fusion(s32[1024]{0:T(1024)} %get-tuple-element.61, bf16[1024,512]{1,0:T(8,128)(2,1)S(1)} %add_convert_fusion, bf16[]{:T(256)} %constant.29.clone.1), kind=kCustom, calls=%fused_computation.71 | custom fusion | bytes 1050112 | tf_op jit(solution)/shard_map/scatter | solution.py:118
  187.7 30.7 %all_to_all.24 = bf16[32,32,512]{2,1,0:T(8,128)(2,1)S(1)} all-to-all(bf16[32,32,512]{2,1,0:T(8,128)(2,1)S(1)} %bitcast.98), channel_id=1, replica_groups=mesh['dp'=32] {'dp'}, dimensions={0} | all-to-all | bytes 2097152 | tf_op jit(solution)/shard_map/all_to_all | solution.py:120
  218.5 5.1 %gather_fusion.1 = bf16[1024,512]{1,0:T(8,128)(2,1)} fusion(bf16[1025,512]{1,0:T(8,128)(2,1)S(1)} %concatenate.11, s32[1024]{0:T(1024)S(1)} %copy-done.21), kind=kCustom, calls=%fused_computation.1 | custom fusion | bytes 2101248 | tf_op jit(solution)/shard_map/gather | solution.py:121
  223.6 33.8 %reduce-scatter.5.cloned.1.call-done = f32[16,512]{1,0:T(8,128)} async-done(((f32[512,512]{1,0:T(8,128)}), f32[16,512]{1,0:T(8,128)}) %reduce-scatter.5.cloned.1.call-update) | async-done | bytes 32784 | tf_op jit(solution)/shard_map/reduce_scatter | solution.py:124
  258.8 139.9 %reduce-scatter.3.cloned.1.call-done = f32[16,2048]{1,0:T(8,128)} async-done(((f32[512,2048]{1,0:T(8,128)}), f32[16,2048]{1,0:T(8,128)}) %reduce-scatter.3.cloned.1.call-update) | async-done | bytes 131088 | tf_op jit(solution)/shard_map/reduce_scatter | solution.py:123
  (94 shorter events, 29.3 us)
Async XLA Ops:
  15.3 33.5 %all-to-all-start = ((bf16[32,32,512]{2,1,0:T(8,128)(2,1)}), bf16[32,32,512]{2,1,0:T(8,128)(2,1)S(1)}, u32[]{:S(2)}, u32[]{:S(2)}) async-start(bf16[32,32,512]{2,1,0:T(8,128)(2,1)} %bitcast), calls=%async_computation | async-start | bytes 2097152 | tf_op jit(solution)/shard_map/all_to_all | solution.py:90
  22.6 234.7 %reduce-scatter.5.cloned.1.call-start = ((), (), s32[]{:S(2)}) async-start(), calls=%async_computation.5 | async-start | bytes 1081344 | tf_op jit(solution)/shard_map/reduce_scatter | solution.py:124
  52.9 9.3 %copy-start.5 = (bf16[1024,512]{1,0:T(8,128)(2,1)}, bf16[1024,512]{1,0:T(8,128)(2,1)S(1)}, u32[]{:S(2)}) copy-start(bf16[1024,512]{1,0:T(8,128)(2,1)S(1)} %gather_fusion) | copy-start | bytes 3145732
  65.3 12.6 %copy-start.7 = (bf16[512,512]{0,1:T(8,128)(2,1)}, bf16[512,512]{0,1:T(8,128)(2,1)S(1)}, u32[]{:S(2)}) copy-start(bf16[512,512]{0,1:T(8,128)(2,1)S(1)} %copy.55) | copy-start | bytes 1572868
  66.8 11.2 %copy-start.9 = (bf16[512,512]{0,1:T(8,128)(2,1)}, bf16[512,512]{0,1:T(8,128)(2,1)S(1)}, u32[]{:S(2)}) copy-start(bf16[512,512]{0,1:T(8,128)(2,1)S(1)} %copy.54) | copy-start | bytes 1572868
  69.3 8.7 %copy-start.3 = (bf16[512,512]{0,1:T(8,128)(2,1)}, bf16[512,512]{0,1:T(8,128)(2,1)S(1)}, u32[]{:S(2)}) copy-start(bf16[512,512]{0,1:T(8,128)(2,1)S(1)} %copy.49) | copy-start | bytes 1572868
  72.2 5.8 %copy-start.15 = (pred[512,1024]{1,0:T(8,128)(4,1)S(1)}, pred[512,1024]{1,0:T(8,128)(4,1)}, u32[]{:S(2)}) copy-start(pred[512,1024]{1,0:T(8,128)(4,1)} %fusion.16) | copy-start | bytes 1572868
  78.0 9.6 %copy-start.13 = (f32[512,8,64]{0,2,1:T(8,128)S(1)}, f32[512,8,64]{0,2,1:T(8,128)}, u32[]{:S(2)}) copy-start(f32[512,8,64]{0,2,1:T(8,128)} %fusion.26) | copy-start | bytes 3145732
  93.9 4.3 %copy-start.11 = (bf16[1024,512]{1,0:T(8,128)(2,1)S(1)}, bf16[1024,512]{1,0:T(8,128)(2,1)}, u32[]{:S(2)}) copy-start(bf16[1024,512]{1,0:T(8,128)(2,1)} %param.13) | copy-start | bytes 3145732
  108.9 3.4 copy-start.17
  112.3 4.7 %copy-start.8 = (bf16[512,512]{0,1:T(8,128)(2,1)S(1)}, bf16[512,512]{0,1:T(8,128)(2,1)}, u32[]{:S(2)}) copy-start(bf16[512,512]{0,1:T(8,128)(2,1)} %copy-done.7) | copy-start | bytes 1572868
  112.3 6.9 %copy-start.10 = (bf16[512,512]{0,1:T(8,128)(2,1)S(1)}, bf16[512,512]{0,1:T(8,128)(2,1)}, u32[]{:S(2)}) copy-start(bf16[512,512]{0,1:T(8,128)(2,1)} %copy-done.9) | copy-start | bytes 1572868
  121.0 277.7 %reduce-scatter.3.cloned.1.call-start = ((), (), s32[]{:S(2)}) async-start(), calls=%async_computation.4 | async-start | bytes 4325376 | tf_op jit(solution)/shard_map/reduce_scatter | solution.py:123
  122.0 5.0 %copy-start.18 = (bf16[512,512]{0,1:T(8,128)(2,1)S(1)}, bf16[512,512]{0,1:T(8,128)(2,1)}, u32[]{:S(2)}) copy-start(bf16[512,512]{0,1:T(8,128)(2,1)} %copy.57) | copy-start | bytes 1572868
  122.0 5.0 %copy-start.22 = (bf16[512,8,64]{0,2,1:T(8,128)(2,1)S(1)}, bf16[512,8,64]{0,2,1:T(8,128)(2,1)}, u32[]{:S(2)}) copy-start(bf16[512,8,64]{0,2,1:T(8,128)(2,1)} %fusion.32) | copy-start | bytes 1572868
  126.2 0.8 copy-start.16
  145.9 7.1 %copy-start.2 = (bf16[8,512,1024]{2,1,0:T(8,128)(2,1)S(1)}, bf16[8,512,1024]{2,1,0:T(8,128)(2,1)}, u32[]{:S(2)}) copy-start(bf16[8,512,1024]{2,1,0:T(8,128)(2,1)} %fusion.2) | copy-start | bytes 25165828
  145.9 7.1 %copy-start.4 = (bf16[512,512]{0,1:T(8,128)(2,1)S(1)}, bf16[512,512]{0,1:T(8,128)(2,1)}, u32[]{:S(2)}) copy-start(bf16[512,512]{0,1:T(8,128)(2,1)} %copy-done.3) | copy-start | bytes 1572868
  145.9 7.1 %copy-start.14 = (bf16[512,8,64]{0,2,1:T(8,128)(2,1)S(1)}, bf16[512,8,64]{0,2,1:T(8,128)(2,1)}, u32[]{:S(2)}) copy-start(bf16[512,8,64]{0,2,1:T(8,128)(2,1)} %fusion.33) | copy-start | bytes 1572868
  153.0 11.0 %copy-start.1 = (f32[1024,512]{1,0:T(8,128)S(1)}, f32[1024,512]{1,0:T(8,128)}, u32[]{:S(2)}) copy-start(f32[1024,512]{1,0:T(8,128)} %get-tuple-element.41) | copy-start | bytes 6291460
  163.9 8.6 %copy-start.6 = (bf16[1024,512]{1,0:T(8,128)(2,1)S(1)}, bf16[1024,512]{1,0:T(8,128)(2,1)}, u32[]{:S(2)}) copy-start(bf16[1024,512]{1,0:T(8,128)(2,1)} %copy-done.5) | copy-start | bytes 3145732
  170.5 2.0 copy-start
  172.5 4.4 %copy-start.12 = (bf16[1024,512]{1,0:T(8,128)(2,1)S(1)}, bf16[1024,512]{1,0:T(8,128)(2,1)}, u32[]{:S(2)}) copy-start(bf16[1024,512]{1,0:T(8,128)(2,1)} %param.13) | copy-start | bytes 3145732
  176.9 41.6 %copy-start.21 = (s32[1024]{0:T(1024)S(1)}, s32[1024]{0:T(1024)}, u32[]{:S(2)}) copy-start(s32[1024]{0:T(1024)} %get-tuple-element.52) | copy-start | bytes 12292
  182.1 75.3 %copy-start.20 = (f32[16,512]{1,0:T(8,128)S(1)}, f32[16,512]{1,0:T(8,128)}, u32[]{:S(2)}) copy-start(f32[16,512]{1,0:T(8,128)} %param.15) | copy-start | bytes 98308
  182.1 216.6 %copy-start.19 = (f32[16,2048]{1,0:T(8,128)S(1)}, f32[16,2048]{1,0:T(8,128)}, u32[]{:S(2)}) copy-start(f32[16,2048]{1,0:T(8,128)} %param.14) | copy-start | bytes 393220
Sparse Core Ops, SparseCore 0:
  121.1 136.2 reduce-scatter.4
  259.6 139.0 reduce-scatter.2
where the time goes:
time: 414 us; the launch traced here: 408 us
  waiting for transfers between devices  195 us (47%)
  matrix products  88.6 us (21%)
  local copies, waits for them, and re-layouts  43.9 us (11%)
  blocking collectives  30.7 us (7%)
  other arithmetic  26.9 us (6%)
  between operations  14.9 us (4%)
  starting transfers between devices  7.41 us (2%)
    reduce_scatter x1, waiting for transfers between devices, shards(): lax.psum_scatter(in_term, 'dp', scatter_dimension=0, tiled=True)  140 us
    dot_general x6, matrix products, attend_pair(): jnp.einsum('hqk,khe->qhe', weights, value_rows, preferred_element_type=jn...  42.3 us
    reduce_scatter x1, waiting for transfers between devices, shards(): lax.psum_scatter(out_term, 'dp', scatter_dimension=0, tiled=True)  33.8 us
    all_to_all x1, blocking collectives, shards(): lax.all_to_all(sendback, 'dp', split_axis=0, concat_axis=0, tiled=True)  30.7 us
    all_to_all x1, waiting for transfers between devices, shards(): lax.all_to_all(outbox, 'dp', split_axis=0, concat_axis=0, tiled=True)  21.4 us
    dot_general x6, matrix products, attend_pair(): jnp.einsum('qhe,khe->hqk', queries, key_rows, preferred_element_type=jnp....  19.5 us
    dot_general x1, matrix products, shards(): hidden = jnp.dot(tokens, w_in, preferred_element_type=jnp.float32)  9.29 us
  transfers between devices with their start and end apart: 3, of which 3 were waited for; matrix products, arithmetic and copies ran while one was open for 18% of the time, Pallas kernels for 0%

commit v1 on v0

v1 whole, which is shorter than its diff:
```python
import functools

import jax
import jax.numpy as jnp
from jax import lax
from jax.experimental import pallas as pl
from jax.experimental.pallas import tpu as pltpu
from jax.sharding import PartitionSpec as P

HEADS = 8
BLK = 512
QB = 256
NORM_EPS = 1e-05
DECAY = 0.9
MESH = pl.DeviceIdType.MESH
F32 = jnp.float32
BF16 = jnp.bfloat16
VMEM_LIMIT = 60 * 1024 * 1024


def dot_nn(a, b):
    return lax.dot_general(a, b, (((1,), (0,)), ((), ())), preferred_element_type=F32)


def dot_nt(a, b):
    return lax.dot_general(a, b, (((1,), (1,)), ((), ())), preferred_element_type=F32)


def dot_tn(a, b):
    return lax.dot_general(a, b, (((0,), (0,)), ((), ())), preferred_element_type=F32)


def chain_bits(bit_count, second):
    order = list(range(bit_count))
    if second and bit_count > 2:
        order[1], order[2] = order[2], order[1]
    return order


def enter_all(n, me):
    barrier = pltpu.get_barrier_semaphore()

    def greet(i, carry):
        pl.semaphore_signal(barrier, inc=1, device_id=((me + i) % n,), device_id_type=MESH)
        return carry

    lax.fori_loop(1, n, greet, 0)
    return barrier


def exchange(n, me, src, dst, ssem, rsem, i):
    peer = (me + i) % n
    return pltpu.make_async_remote_copy(
        src_ref=src.at[peer],
        dst_ref=dst.at[me],
        send_sem=ssem.at[i],
        recv_sem=rsem.at[i],
        device_id=(peer,),
        device_id_type=MESH,
    )


def start_exchange(n, me, src, dst, ssem, rsem):
    def go(i, carry):
        exchange(n, me, src, dst, ssem, rsem, i).start()
        return carry

    lax.fori_loop(n // 2, n, go, 0)
    lax.fori_loop(1, n // 2, go, 0)


def finish_exchange(n, me, src, dst, ssem, rsem):
    def end(i, carry):
        exchange(n, me, src, dst, ssem, rsem, i).wait()
        return carry

    lax.fori_loop(1, n, end, 0)


def gather_matrix(slots_ref, out_ref):
    rows = out_ref.shape[0]
    wide = jnp.broadcast_to(slots_ref[...].astype(F32), (128, rows))
    column = jnp.transpose(wide)
    lane = lax.broadcasted_iota(jnp.int32, (rows, 128), 1).astype(F32)
    for j in range(rows // 128):
        out_ref[:, j * 128 : (j + 1) * 128] = jnp.where(
            column == lane + float(j * 128), 1.0, 0.0
        ).astype(BF16)


def scatter_chunk(slots_ref, start, size):
    rows = slots_ref.shape[1]
    place = lax.broadcasted_iota(jnp.int32, (size, rows), 0) + start
    return jnp.where(place == slots_ref[...], 1.0, 0.0).astype(BF16)


def inbound_kernel(n, home_ref, dest_ref, ev_ref, tok_ref, outbox, inbox, pick, ssem, rsem):
    me = lax.axis_index("dp")
    rows, width = ev_ref.shape
    cap = rows // n
    barrier = enter_all(n, me)
    step = 256
    group = step // cap

    def fill(c, carry):
        part = dot_nn(scatter_chunk(home_ref, c * step, step), ev_ref[...]).astype(BF16)
        outbox[pl.ds(c * group, group)] = part.reshape(group, cap, width)
        return carry

    lax.fori_loop(0, rows // step, fill, 0)
    pl.semaphore_wait(barrier, n - 1)
    start_exchange(n, me, outbox, inbox, ssem, rsem)
    inbox[me] = outbox[me]
    gather_matrix(dest_ref, pick)
    finish_exchange(n, me, outbox, inbox, ssem, rsem)
    for c in range(rows // step):
        tok_ref[c * step : (c + 1) * step] = dot_nn(
            pick[c * step : (c + 1) * step], inbox[...].reshape(rows, width)
        ).astype(BF16)


def owner_of(place, lens_ref, none):
    owner = jnp.full(place.shape, none, jnp.int32)
    start = 0
    for j in range(lens_ref.shape[0]):
        length = lens_ref[j]
        inside = (place >= start) & (place < start + length)
        owner = jnp.where(inside, j, owner)
        start = start + (length + BLK - 1) // BLK * BLK
    return owner


def order_matrix(shape, n, per, bits):
    width = shape[1]
    place = lax.broadcasted_iota(jnp.int32, shape, 0)
    column = lax.broadcasted_iota(jnp.int32, shape, 1)
    slot = place // per
    device = jnp.zeros(shape, jnp.int32)
    for rank, bit in enumerate(bits):
        weight = n >> (rank + 1)
        device = device + ((slot // weight) % 2) * (1 << bit)
    return jnp.where(column == device * per + place % per, 1.0, 0.0).astype(BF16)


def layer_kernel(
    n, lens_ref, dest_ref, tok_ref, w_ref, og_ref,
    back_ref, ga_ref, gb_ref,
    slope, gate, qs, ks, vs, att, hgrad, mask, mask_t, mixed, dout, tgrad, acc_k, acc_v, tp,
):
    rows, width = tok_ref.shape
    per = width // n
    nq = rows // QB
    bits = n.bit_length() - 1

    def project(c, carry):
        r = pl.ds(pl.multiple_of(c * QB, QB), QB)
        x = tok_ref[r, :]
        for g in range(4):
            cols = slice(g * width, (g + 1) * width)
            u = dot_nn(x, w_ref[:, cols]) * 0.5
            t = jnp.tanh(u)
            a = u * t + u
            slope[r, cols] = 0.5 * ((1.0 + a) + t * (1.0 - a))
            if g == 0:
                gate[r, :] = a
            elif g == 1:
                vs[r, :] = a.astype(BF16)
            elif g == 2:
                qs[r, :] = (a.astype(BF16).astype(F32) * (0.5 * (width // HEADS) ** -0.5)).astype(BF16)
            else:
                ks[r, :] = a.astype(BF16)
        low = lax.broadcasted_iota(jnp.int32, (QB, rows), 0) + c * QB
        high = lax.broadcasted_iota(jnp.int32, (QB, rows), 1)
        low_col = lax.broadcasted_iota(jnp.int32, (QB, 1), 0) + c * QB
        high_row = lax.broadcasted_iota(jnp.int32, (1, rows), 1)
        q_own = owner_of(low_col, lens_ref, -1)
        k_own = owner_of(high_row, lens_ref, -2)
        mask[r, :] = jnp.where((q_own == k_own) & (high <= low), 1.0, 0.0).astype(BF16)
        mask_t[r, :] = jnp.where((q_own == k_own) & (low <= high), 1.0, 0.0).astype(BF16)
        return carry

    lax.fori_loop(0, nq, project, 0)

    pair_width = 128
    head = width // HEADS
    lane = lax.broadcasted_iota(jnp.int32, (1, pair_width), 1) // head
    picks = [jnp.where(lane == h, 1.0, 0.0).astype(BF16) for h in range(pair_width // head)]

    def forward(p, carry):
        cols = pl.ds(pl.multiple_of(p * pair_width, pair_width), pair_width)
        for c in range(nq):
            top = (c + 1) * QB
            r = slice(c * QB, top)
            out = None
            for sel in picks:
                u = dot_nt(qs[r, cols] * sel, ks[:top, cols])
                t = jnp.tanh(u)
                a = (u * t + u).astype(BF16) * mask[r, :top]
                o = dot_nn(a, vs[:top, cols] * sel)
                out = o if out is None else out + o
            att[r, cols] = out
        return carry

    lax.fori_loop(0, width // pair_width, forward, 0)

    def norm(c, carry):
        r = pl.ds(pl.multiple_of(c * QB, QB), QB)
        x = att[r, :]
        centred = x - jnp.mean(x, axis=1, keepdims=True)
        spread = jnp.mean(centred * centred, axis=1, keepdims=True)
        inv = lax.rsqrt(spread + NORM_EPS)
        unit = centred * inv
        g = gate[r, :]
        mixed[r, :] = (unit * g).astype(BF16)
        dmix = dot_nt(og_ref[r, :], w_ref[:, 4 * width :])
        hgrad[r, :width] = (dmix * unit * slope[r, :width]).astype(BF16)
        dn = dmix * g
        mean_a = jnp.mean(dn, axis=1, keepdims=True)
        mean_b = jnp.mean(dn * unit, axis=1, keepdims=True)
        dout[r, :] = (inv * (dn - mean_a - unit * mean_b)).astype(BF16)
        return carry

    lax.fori_loop(0, nq, norm, 0)

    def backward(p, carry):
        off = pl.multiple_of(p * pair_width, pair_width)
        cols = pl.ds(off, pair_width)
        for c in range(nq):
            top = (c + 1) * QB
            r = slice(c * QB, top)
            dq = None
            for sel in picks:
                qm = qs[r, cols] * sel
                dm = dout[r, cols] * sel
                u = dot_nt(ks[:top, cols], qm)
                t = jnp.tanh(u)
                a = u * t + u
                m = mask_t[:top, r]
                d = dot_nt(vs[:top, cols], dm)
                ds = (d * ((1.0 + a) + t * (1.0 - a))).astype(BF16) * m
                pb = a.astype(BF16) * m
                dv = dot_nn(pb, dm)
                dk = dot_nn(ds, qm)
                part = dot_tn(ds, ks[:top, cols] * sel)
                dq = part if dq is None else dq + part
                if c > 0:
                    acc_v[: c * QB, :] += dv[: c * QB]
                    acc_k[: c * QB, :] += dk[: c * QB]
                if sel is picks[0]:
                    acc_v[c * QB : top, :] = dv[c * QB :]
                    acc_k[c * QB : top, :] = dk[c * QB :]
                else:
                    acc_v[c * QB : top, :] += dv[c * QB :]
                    acc_k[c * QB : top, :] += dk[c * QB :]
            qcols = pl.ds(2 * width + off, pair_width)
            dq = (dq * (0.5 * head**-0.5)).astype(BF16).astype(F32)
            hgrad[r, qcols] = (dq * slope[r, qcols]).astype(BF16)
        vcols = pl.ds(width + off, pair_width)
        kcols = pl.ds(3 * width + off, pair_width)
        hgrad[:, vcols] = (acc_v[...].astype(BF16).astype(F32) * slope[:, vcols]).astype(BF16)
        hgrad[:, kcols] = (acc_k[...].astype(BF16).astype(F32) * slope[:, kcols]).astype(BF16)
        return carry

    lax.fori_loop(0, width // pair_width, backward, 0)

    def tokens_back(c, carry):
        r = pl.ds(pl.multiple_of(c * QB, QB), QB)
        tgrad[r, :] = (
            og_ref[r, :].astype(F32) + dot_nt(hgrad[r, :], w_ref[:, : 4 * width])
        ).astype(BF16)
        return carry

    lax.fori_loop(0, nq, tokens_back, 0)
    cap = rows // n
    group = QB // cap

    def send_rows(c, carry):
        part = dot_nn(scatter_chunk(dest_ref, c * QB, QB), tgrad[...]).astype(BF16)
        back_ref[pl.ds(c * group, group)] = part.reshape(group, cap, width)
        return carry

    lax.fori_loop(0, nq, send_rows, 0)

    half = ga_ref.shape[1]
    step = 256
    for ref, base, second in ((ga_ref, 0, False), (gb_ref, half, True)):
        order = order_matrix((width, width), n, per, chain_bits(bits, second))
        tp[...] = dot_nt(order, tok_ref[...]).astype(BF16)

        def columns(j, carry, ref=ref, base=base):
            src = pl.ds(pl.multiple_of(base + j * step, 128), step)
            dst = pl.ds(pl.multiple_of(j * step, 128), step)
            ref[:, dst] = dot_nn(tp[...], hgrad[:, src]).astype(BF16)
            return carry

        wide = min(half, 4 * width - base)
        lax.fori_loop(0, wide // step, columns, 0)
    tp[...] = dot_nt(order, mixed[...]).astype(BF16)
    gb_ref[:, wide:] = dot_nn(tp[...], og_ref[...]).astype(BF16)


def outbound_kernel(n, home_ref, back_ref, ga_ref, gb_ref, ev_ref, fa_ref, fb_ref, *scratch):
    bits = n.bit_length() - 1
    inbox, pick, ssem, rsem, hs, hr = scratch[:6]
    bufs = scratch[6:]
    me = lax.axis_index("dp")
    rows = pick.shape[0]
    width = inbox.shape[2]
    barrier = enter_all(n, me)
    pl.semaphore_wait(barrier, n - 1)

    def hop(chain, stage):
        bit = chain_bits(bits, chain == 1)[stage]
        mine = (me // (1 << bit)) % 2
        peer = me + (1 - 2 * mine) * (1 << bit)
        cur = (ga_ref, gb_ref)[chain] if stage == 0 else bufs[(chain * bits + stage - 1) * 2 + 1]
        got = bufs[(chain * bits + stage) * 2]
        half = cur.shape[0] // 2
        copy = pltpu.make_async_remote_copy(
            src_ref=cur.at[pl.ds((1 - mine) * half, half)],
            dst_ref=got,
            send_sem=hs.at[chain * bits + stage],
            recv_sem=hr.at[chain * bits + stage],
            device_id=(peer,),
            device_id_type=MESH,
        )
        return copy, cur.at[pl.ds(mine * half, half)], got

    live = [hop(0, 0), hop(1, 0)]
    for copy, _, _ in live:
        copy.start()
    start_exchange(n, me, back_ref, inbox, ssem, rsem)
    inbox[me] = back_ref[me]
    gather_matrix(home_ref, pick)
    for stage in range(bits):
        for chain in range(2):
            copy, kept, got = live[chain]
            copy.wait()
            total = kept[...].astype(F32) + got[...].astype(F32)
            if stage == bits - 1:
                (fa_ref, fb_ref)[chain][...] = total
            else:
                bufs[(chain * bits + stage) * 2 + 1][...] = total.astype(BF16)
                live[chain] = hop(chain, stage + 1)
                live[chain][0].start()
    finish_exchange(n, me, back_ref, inbox, ssem, rsem)
    step = 256
    for c in range(rows // step):
        ev_ref[c * step : (c + 1) * step] = dot_nn(
            pick[c * step : (c + 1) * step], inbox[...].reshape(rows, width)
        ).astype(BF16)


def shards(n, events, home_slot, dest_slot, seq_lens, weights, out_grad, momentum_in, momentum_out):
    rows, width = events.shape
    cap = rows // n
    bits = n.bit_length() - 1
    per = width // n
    home = home_slot.reshape(1, rows)
    dest = dest_slot.reshape(1, rows)
    vm = pl.BlockSpec(memory_space=pltpu.VMEM)
    sm = pl.BlockSpec(memory_space=pltpu.SMEM)
    dma = pltpu.SemaphoreType.DMA
    tokens = pl.pallas_call(
        functools.partial(inbound_kernel, n),
        out_shape=jax.ShapeDtypeStruct((rows, width), BF16),
        in_specs=[vm] * 3,
        out_specs=vm,
        scratch_shapes=[
            pltpu.VMEM((n, cap, width), BF16),
            pltpu.VMEM((n, cap, width), BF16),
            pltpu.VMEM((rows, rows), BF16),
            dma((n,)),
            dma((n,)),
        ],
        compiler_params=pltpu.CompilerParams(
            collective_id=0, has_side_effects=True, vmem_limit_bytes=VMEM_LIMIT
        ),
        name="inbound",
    )(home, dest, events)
    half = 5 * width // 2
    back, ga, gb = pl.pallas_call(
        functools.partial(layer_kernel, n),
        out_shape=[
            jax.ShapeDtypeStruct((n, cap, width), BF16),
            jax.ShapeDtypeStruct((width, half), BF16),
            jax.ShapeDtypeStruct((width, half), BF16),
        ],
        in_specs=[sm, vm, vm, vm, vm],
        out_specs=[vm] * 3,
        scratch_shapes=[
            pltpu.VMEM((rows, 4 * width), F32),
            pltpu.VMEM((rows, width), F32),
            pltpu.VMEM((rows, width), BF16),
            pltpu.VMEM((rows, width), BF16),
            pltpu.VMEM((rows, width), BF16),
            pltpu.VMEM((rows, width), F32),
            pltpu.VMEM((rows, 4 * width), BF16),
            pltpu.VMEM((rows, rows), BF16),
            pltpu.VMEM((rows, rows), BF16),
            pltpu.VMEM((rows, width), BF16),
            pltpu.VMEM((rows, width), BF16),
            pltpu.VMEM((rows, width), BF16),
            pltpu.VMEM((rows, 128), F32),
            pltpu.VMEM((rows, 128), F32),
            pltpu.VMEM((width, rows), BF16),
        ],
        compiler_params=pltpu.CompilerParams(vmem_limit_bytes=VMEM_LIMIT),
        name="layer",
    )(seq_lens, dest, tokens, weights, out_grad)
    tall = max(per, 16)
    thin = half * per // tall
    ga = ga.reshape(n * tall, thin)
    gb = gb.reshape(n * tall, thin)
    bufs = []
    for chain in range(2):
        for stage in range(bits):
            size = (n * tall >> (stage + 1), thin)
            bufs += [pltpu.VMEM(size, BF16), pltpu.VMEM(size, BF16)]
    event_grad, fa, fb = pl.pallas_call(
        functools.partial(outbound_kernel, n),
        out_shape=[
            jax.ShapeDtypeStruct((rows, width), BF16),
            jax.ShapeDtypeStruct((tall, thin), F32),
            jax.ShapeDtypeStruct((tall, thin), F32),
        ],
        in_specs=[vm] * 4,
        out_specs=[vm] * 3,
        scratch_shapes=[
            pltpu.VMEM((n, cap, width), BF16),
            pltpu.VMEM((rows, rows), BF16),
            dma((n,)),
            dma((n,)),
            dma((2 * bits,)),
            dma((2 * bits,)),
        ]
        + bufs,
        compiler_params=pltpu.CompilerParams(
            collective_id=1, has_side_effects=True, vmem_limit_bytes=VMEM_LIMIT
        ),
        name="outbound",
    )(home, back, ga, gb)
    sums = jnp.concatenate([fa.reshape(per, half), fb.reshape(per, half)], axis=1)
    grad_scale = (n * rows) ** (-0.5)
    return (
        event_grad,
        DECAY * momentum_in + grad_scale * sums[:, : 4 * width],
        DECAY * momentum_out + grad_scale * sums[:, 4 * width :],
    )


def solution(mesh):
    n = mesh.shape["dp"]
    row = P("dp", None)
    return jax.shard_map(
        functools.partial(shards, n),
        mesh=mesh,
        in_specs=(row, P("dp"), P("dp"), P("dp"), P(), row, row, row),
        out_specs=(row, row, row),
        check_vma=False,
    )
```

time: 414 us -> 135 us (0.33); the launches traced: 408 us -> 134 us
  waiting for transfers between devices: 195 us -> 0 us
  Pallas kernels: 0 us -> 129 us
  matrix products: 88.6 us -> 0 us
  local copies, waits for them, and re-layouts: 43.9 us -> 2.27 us
  blocking collectives: 30.7 us -> 0 us
  other arithmetic: 26.9 us -> 2.98 us
  between operations: 14.9 us -> 0.66 us
  starting transfers between devices: 7.41 us -> 0 us
    reduce_scatter x2 -> x0, waiting for transfers between devices: 174 us -> none  [the longest x1 140 us: shards(): lax.psum_scatter(in_term, 'dp', scatter_dimension=0, tiled=True)]
    pallas_call x0 -> x3, Pallas kernels: none -> 129 us  [the longest x1 48.8 us: shards(): pl.pallas_call(functools.partial(layer_kernel, n), out_shape=[jax.ShapeDt...]
    dot_general x17 -> x0, matrix products: 88.6 us -> none  [the longest x6 42.3 us: attend_pair(): jnp.einsum('hqk,khe->qhe', weights, value_rows, preferred_element_type=jn...]
    all_to_all x1 -> x0, blocking collectives: 30.7 us -> none  [shards(): lax.all_to_all(sendback, 'dp', split_axis=0, concat_axis=0, tiled=True)]
    all_to_all x1 -> x0, waiting for transfers between devices: 21.4 us -> none  [shards(): lax.all_to_all(outbox, 'dp', split_axis=0, concat_axis=0, tiled=True)]
    scatter x2 -> x0, local copies, waits for them, and re-layouts: 11.3 us -> none  [the longest x1 5.81 us: shards(): jnp.zeros((row_count + 1, model_width), jnp.bfloat16).at[home_slot]]
    slice x13 -> x0, local copies, waits for them, and re-layouts: 11.1 us -> none  [the longest x1 2.9 us: mixing(): activated[:, model_width:2 * model_width].astype(jnp.bfloat16)]
    gather x2 -> x0, local copies, waits for them, and re-layouts: 9.05 us -> none  [the longest x1 5.08 us: shards(): event_grad = jnp.concatenate([returned, zero_row], axis=0)[home_slot]]
  transfers between devices with their start and end apart: 3 -> 0, of which waited for: 3 -> 0; matrix products, arithmetic and copies ran while one was open for 18% -> 0% of each run, Pallas kernels for 0% -> 0%
where the time goes in v1:
time: 135 us; the launch traced here: 134 us
  Pallas kernels  129 us (96%)
  other arithmetic  2.98 us (2%)
  local copies, waits for them, and re-layouts  2.27 us (2%)
    pallas_call x1, Pallas kernels, shards(): pl.pallas_call(functools.partial(layer_kernel, n), out_shape=[jax.ShapeDt...  48.8 us
    pallas_call x1, Pallas kernels, shards(): pl.pallas_call(functools.partial(outbound_kernel, n), out_shape=[jax.Shap...  44.8 us
    pallas_call x1, Pallas kernels, shards(): pl.pallas_call(functools.partial(inbound_kernel, n), out_shape=jax.ShapeD...  35 us

profile of v1, /device:TPU:0, one launch (start us, length us, event | category | flops | bytes accessed | tf_op | source)
XLA Modules:
  0.0 134.4 jit_solution(17989314326470622791)
XLA Ops:
  0.6 35.0 %inbound.1.tok_ref = bf16[1024,512]{1,0:T(8,128)(2,1)} custom-call(s32[1,1024]{1,0:T(1,128)} %bitcast.4, s32[1,1024]{1,0:T(1,128)} %bitcast.2, bf16[1024,512]{1,0:T(8,128)(2,1)} %ev_ref.1), custom_call_target="tpu_custom_call" | custom-call | tf_op jit(solution)/shard_map/inbound/pallas_call | solution.py:364
  35.6 48.8 %layer.1 = (bf16[32,32,512]{2,1,0:T(8,128)(2,1)}, bf16[512,1280]{1,0:T(8,128)(2,1)}, bf16[512,1280]{1,0:T(8,128)(2,1)}) custom-call(s32[2]{0:T(128)} %lens_ref.1, s32[1,1024]{1,0:T(1,128)} %bitcast.3, bf16[1024,512]{1,0:T(8,128)(2,1)} %inbound.1.tok_ref, bf16[512,2560]{1,0:T(8,128)(2,1)} %w_ref.1, bf16[1024,512]{1,0:T(8,128)(2,1)} %og_ref.1), custom_call_target="tpu_custom_call" | custom-call | tf_op jit(solution)/shard_map/layer/pallas_call | solution.py:382
  84.4 0.0 copy-start.1
  84.4 0.0 copy-start
  84.4 44.8 %outbound.1 = (bf16[1024,512]{1,0:T(8,128)(2,1)}, f32[16,1280]{1,0:T(8,128)}, f32[16,1280]{1,0:T(8,128)}) custom-call(s32[1,1024]{1,0:T(1,128)} %bitcast.5, bf16[32,32,512]{2,1,0:T(8,128)(2,1)} %get-tuple-element.9.back_ref, bf16[512,1280]{1,0:T(8,128)(2,1)} %get-tuple-element.10.ga_ref, bf16[512,1280]{1,0:T(8,128)(2,1)} %get-tuple-element.11.gb_ref), custom_call_target="tpu_custom_call" | custom-call | tf_op jit(solution)/shard_map/outbound/pallas_call | solution.py:420
  129.2 0.0 copy-done.1
  129.2 1.4 %multiply_add_fusion = f32[16,512]{1,0:T(8,128)} fusion(f32[16,1280]{1,0:T(8,128)} %get-tuple-element.14, f32[16,512]{1,0:T(8,128)S(1)} %copy-done.1), kind=kLoop, calls=%fused_computation.3 | loop fusion | flops 24576 | bytes 98304 | tf_op jit(solution)/shard_map/add | solution.py:448
  130.6 0.0 copy-done
  130.6 1.6 %fusion.1 = f32[16,2048]{1,0:T(8,128)} fusion(f32[16,1280]{1,0:T(8,128)} %get-tuple-element.14, f32[16,1280]{1,0:T(8,128)} %get-tuple-element.13, f32[16,2048]{1,0:T(8,128)S(1)} %copy-done), kind=kLoop, calls=%fused_computation.2 | loop fusion | flops 131072 | bytes 425984 | tf_op jit(solution)/shard_map/add | solution.py:447
  132.2 2.3 %copy.12 = bf16[1024,512]{1,0:T(8,128)(2,1)} copy(bf16[1024,512]{1,0:T(8,128)(2,1)} %get-tuple-element.18) | data formatting | bytes 2097152
Async XLA Ops:
  84.4 44.8 %copy-start.1 = (f32[16,512]{1,0:T(8,128)S(1)}, f32[16,512]{1,0:T(8,128)}, u32[]{:S(2)}) copy-start(f32[16,512]{1,0:T(8,128)} %param.15) | copy-start | bytes 98308
  84.4 46.2 %copy-start = (f32[16,2048]{1,0:T(8,128)S(1)}, f32[16,2048]{1,0:T(8,128)}, u32[]{:S(2)}) copy-start(f32[16,2048]{1,0:T(8,128)} %param.14) | copy-start | bytes 393220

commit v2 on v1

v2 whole, which is shorter than its diff:
```python
import functools

import jax
import jax.numpy as jnp
from jax import lax
from jax.experimental import pallas as pl
from jax.experimental.pallas import tpu as pltpu
from jax.sharding import PartitionSpec as P

HEADS = 8
BLK = 512
QB = 256
NORM_EPS = 1e-05
DECAY = 0.9
MESH = pl.DeviceIdType.MESH
F32 = jnp.float32
BF16 = jnp.bfloat16
VMEM_LIMIT = 66 * 1000 * 1000


def dot_nn(a, b):
    return lax.dot_general(a, b, (((1,), (0,)), ((), ())), preferred_element_type=F32)


def dot_nt(a, b):
    return lax.dot_general(a, b, (((1,), (1,)), ((), ())), preferred_element_type=F32)


def dot_tn(a, b):
    return lax.dot_general(a, b, (((0,), (0,)), ((), ())), preferred_element_type=F32)


def chain_bits(bit_count, second):
    order = list(range(bit_count))
    if second and bit_count > 2:
        order[1], order[2] = order[2], order[1]
    return order


def enter_all(n, me):
    barrier = pltpu.get_barrier_semaphore()

    def greet(i, carry):
        pl.semaphore_signal(barrier, inc=1, device_id=((me + i) % n,), device_id_type=MESH)
        return carry

    lax.fori_loop(1, n, greet, 0)
    return barrier


def exchange(n, me, src, dst, ssem, rsem, i):
    peer = (me + i) % n
    return pltpu.make_async_remote_copy(
        src_ref=src.at[peer],
        dst_ref=dst.at[me],
        send_sem=ssem.at[i],
        recv_sem=rsem.at[i],
        device_id=(peer,),
        device_id_type=MESH,
    )


def start_exchange(n, me, src, dst, ssem, rsem):
    def go(i, carry):
        exchange(n, me, src, dst, ssem, rsem, i).start()
        return carry

    lax.fori_loop(n // 2, n, go, 0)
    lax.fori_loop(1, n // 2, go, 0)


def finish_exchange(n, me, src, dst, ssem, rsem):
    def end(i, carry):
        exchange(n, me, src, dst, ssem, rsem, i).wait()
        return carry

    lax.fori_loop(1, n, end, 0)


def gather_matrix(slots_ref, out_ref):
    rows = out_ref.shape[0]
    wide = jnp.broadcast_to(slots_ref[...].astype(F32), (128, rows))
    column = jnp.transpose(wide)
    lane = lax.broadcasted_iota(jnp.int32, (rows, 128), 1).astype(F32)
    for j in range(rows // 128):
        out_ref[:, j * 128 : (j + 1) * 128] = jnp.where(
            column == lane + float(j * 128), 1.0, 0.0
        ).astype(BF16)


def scatter_chunk(slots_ref, start, size):
    rows = slots_ref.shape[1]
    place = lax.broadcasted_iota(jnp.int32, (size, rows), 0) + start
    return jnp.where(place == slots_ref[...], 1.0, 0.0).astype(BF16)


def owner_of(place, lens_ref, none):
    owner = jnp.full(place.shape, none, jnp.int32)
    start = 0
    for j in range(lens_ref.shape[0]):
        length = lens_ref[j]
        inside = (place >= start) & (place < start + length)
        owner = jnp.where(inside, j, owner)
        start = start + (length + BLK - 1) // BLK * BLK
    return owner


def order_matrix(height, width, n, per, bits, fold, turn):
    shape = (height, width)
    tall = per * fold
    place = lax.broadcasted_iota(jnp.int32, shape, 0)
    column = lax.broadcasted_iota(jnp.int32, shape, 1)
    slot = place // tall
    rest = place % tall
    device = jnp.zeros(shape, jnp.int32)
    for rank, bit in enumerate(bits):
        weight = n >> (rank + 1)
        device = device + ((slot // weight) % 2) * (1 << bit)
    hit = (column == device * per + rest % per) & (rest // per == turn)
    return jnp.where(hit, 1.0, 0.0).astype(BF16)


def step_kernel(
    n, lens_ref, home_ref, dest_ref, ev_ref, w_hbm, og_hbm,
    ret_ref, f0_ref, f1_ref, f2_ref, f3_ref,
    w_ref, og_ref, outbox, inbox, inbox2, pick, tok_ref, dmix,
    slope, gate, qs, ks, vs, att, hgrad, mask, mask_t, mixed, dout, acc_k, acc_v, tp,
    lsem, ssem, rsem, ssem2, rsem2, hs, hr, *bufs,
):
    me = lax.axis_index("dp")
    rows, width = ev_ref.shape
    cap = rows // n
    per = width // n
    fold = max(1, 16 // per)
    nq = rows // QB
    bits = n.bit_length() - 1
    group = QB // cap
    barrier = enter_all(n, me)
    load_w = pltpu.make_async_copy(w_hbm, w_ref, lsem.at[0])
    load_og = pltpu.make_async_copy(og_hbm, og_ref, lsem.at[1])
    load_w.start()
    load_og.start()

    def fill(c, carry):
        part = dot_nn(scatter_chunk(home_ref, c * QB, QB), ev_ref[...]).astype(BF16)
        outbox[pl.ds(c * group, group)] = part.reshape(group, cap, width)
        return carry

    lax.fori_loop(0, nq, fill, 0)
    pl.semaphore_wait(barrier, n - 1)
    start_exchange(n, me, outbox, inbox, ssem, rsem)
    inbox[me] = outbox[me]
    gather_matrix(dest_ref, pick)
    load_w.wait()
    load_og.wait()

    def prepare(c, carry):
        r = pl.ds(pl.multiple_of(c * QB, QB), QB)
        low = lax.broadcasted_iota(jnp.int32, (QB, rows), 0) + c * QB
        high = lax.broadcasted_iota(jnp.int32, (QB, rows), 1)
        low_col = lax.broadcasted_iota(jnp.int32, (QB, 1), 0) + c * QB
        high_row = lax.broadcasted_iota(jnp.int32, (1, rows), 1)
        q_own = owner_of(low_col, lens_ref, -1)
        k_own = owner_of(high_row, lens_ref, -2)
        mask[r, :] = jnp.where((q_own == k_own) & (high <= low), 1.0, 0.0).astype(BF16)
        mask_t[r, :] = jnp.where((q_own == k_own) & (low <= high), 1.0, 0.0).astype(BF16)
        dmix[r, :] = dot_nt(og_ref[r, :], w_ref[:, 4 * width :]).astype(BF16)
        return carry

    lax.fori_loop(0, nq, prepare, 0)
    finish_exchange(n, me, outbox, inbox, ssem, rsem)

    def project(c, carry):
        r = pl.ds(pl.multiple_of(c * QB, QB), QB)
        x = dot_nn(pick[r, :], inbox[...].reshape(rows, width)).astype(BF16)
        tok_ref[r, :] = x
        for g in range(4):
            cols = slice(g * width, (g + 1) * width)
            u = dot_nn(x, w_ref[:, cols]) * 0.5
            t = jnp.tanh(u)
            a = u * t + u
            slope[r, cols] = (0.5 * ((1.0 + a) + t * (1.0 - a))).astype(BF16)
            if g == 0:
                gate[r, :] = a
            elif g == 1:
                vs[r, :] = a.astype(BF16)
            elif g == 2:
                qs[r, :] = (a.astype(BF16).astype(F32) * (0.5 * (width // HEADS) ** -0.5)).astype(BF16)
            else:
                ks[r, :] = a.astype(BF16)
        return carry

    lax.fori_loop(0, nq, project, 0)

    pair_width = 128
    head = width // HEADS
    lane = lax.broadcasted_iota(jnp.int32, (1, pair_width), 1) // head
    picks = [jnp.where(lane == h, 1.0, 0.0).astype(BF16) for h in range(pair_width // head)]

    def forward(p, carry):
        cols = pl.ds(pl.multiple_of(p * pair_width, pair_width), pair_width)
        for c in range(nq):
            top = (c + 1) * QB
            r = slice(c * QB, top)
            out = None
            for sel in picks:
                u = dot_nt(qs[r, cols] * sel, ks[:top, cols])
                t = jnp.tanh(u)
                a = (u * t + u).astype(BF16) * mask[r, :top]
                o = dot_nn(a, vs[:top, cols] * sel)
                out = o if out is None else out + o
            att[r, cols] = out
        return carry

    lax.fori_loop(0, width // pair_width, forward, 0)

    def norm(c, carry):
        r = pl.ds(pl.multiple_of(c * QB, QB), QB)
        x = att[r, :]
        centred = x - jnp.mean(x, axis=1, keepdims=True)
        spread = jnp.mean(centred * centred, axis=1, keepdims=True)
        inv = lax.rsqrt(spread + NORM_EPS)
        unit = centred * inv
        g = gate[r, :]
        mixed[r, :] = (unit * g).astype(BF16)
        dm = dmix[r, :].astype(F32)
        hgrad[r, :width] = (dm * unit * slope[r, :width]).astype(BF16)
        dn = dm * g
        mean_a = jnp.mean(dn, axis=1, keepdims=True)
        mean_b = jnp.mean(dn * unit, axis=1, keepdims=True)
        dout[r, :] = (inv * (dn - mean_a - unit * mean_b)).astype(BF16)
        return carry

    lax.fori_loop(0, nq, norm, 0)

    pairs = width // pair_width
    sources = bufs[:4]
    hops = bufs[4:]
    sums = (f0_ref, f1_ref, f2_ref, f3_ref)

    def hop(chain, stage):
        bit = chain_bits(bits, chain % 2 == 1)[stage]
        mine = (me // (1 << bit)) % 2
        peer = me + (1 - 2 * mine) * (1 << bit)
        cur = sources[chain] if stage == 0 else hops[chain * bits + stage - 1]
        got = hops[chain * bits + stage]
        half = cur.shape[0] // 2
        copy = pltpu.make_async_remote_copy(
            src_ref=cur.at[pl.ds((1 - mine) * half, half)],
            dst_ref=got,
            send_sem=hs.at[chain * bits + stage],
            recv_sem=hr.at[chain * bits + stage],
            device_id=(peer,),
            device_id_type=MESH,
        )
        return copy, cur.at[pl.ds(mine * half, half)], got

    def advance(chain, stage):
        copy, kept, got = hop(chain, stage)
        copy.wait()
        total = kept[...].astype(F32) + got[...].astype(F32)
        if stage == bits - 1:
            sums[chain][...] = total
        else:
            got[...] = total.astype(BF16)
            hop(chain, stage + 1)[0].start()

    def weight_grad(chain, left, right, base, wide):
        thin = wide // fold
        height = n * per * fold
        order = chain_bits(bits, chain % 2 == 1)
        for turn in range(fold):
            tp[...] = dot_nt(
                order_matrix(height, width, n, per, order, fold, turn), left[...]
            ).astype(BF16)
            step = 256 if thin % 256 == 0 else thin
            for j in range(thin // step):
                start = base + turn * thin + j * step
                part = dot_nn(tp[...], right[:, start : start + step])
                cols = slice(j * step, (j + 1) * step)
                if turn == 0:
                    sources[chain][:, cols] = part.astype(BF16)
                else:
                    sources[chain][:, cols] += part.astype(BF16)
        hop(chain, 0)[0].start()

    weight_grad(0, tok_ref, hgrad, 0, width)
    weight_grad(1, mixed, og_ref, 0, width)

    def backward(p, carry):
        off = pl.multiple_of(p * pair_width, pair_width)
        cols = pl.ds(off, pair_width)
        for c in range(nq):
            top = (c + 1) * QB
            r = slice(c * QB, top)
            dq = None
            for sel in picks:
                qm = qs[r, cols] * sel
                dm = dout[r, cols] * sel
                u = dot_nt(ks[:top, cols], qm)
                t = jnp.tanh(u)
                a = u * t + u
                m = mask_t[:top, r]
                d = dot_nt(vs[:top, cols], dm)
                ds = (d * ((1.0 + a) + t * (1.0 - a))).astype(BF16) * m
                pb = a.astype(BF16) * m
                dv = dot_nn(pb, dm)
                dk = dot_nn(ds, qm)
                part = dot_tn(ds, ks[:top, cols] * sel)
                dq = part if dq is None else dq + part
                if c > 0:
                    acc_v[: c * QB, :] += dv[: c * QB]
                    acc_k[: c * QB, :] += dk[: c * QB]
                if sel is picks[0]:
                    acc_v[c * QB : top, :] = dv[c * QB :]
                    acc_k[c * QB : top, :] = dk[c * QB :]
                else:
                    acc_v[c * QB : top, :] += dv[c * QB :]
                    acc_k[c * QB : top, :] += dk[c * QB :]
            qcols = pl.ds(2 * width + off, pair_width)
            dq = (dq * (0.5 * head**-0.5)).astype(BF16).astype(F32)
            hgrad[r, qcols] = (dq * slope[r, qcols]).astype(BF16)
        vcols = pl.ds(width + off, pair_width)
        kcols = pl.ds(3 * width + off, pair_width)
        hgrad[:, vcols] = (acc_v[...].astype(BF16).astype(F32) * slope[:, vcols]).astype(BF16)
        hgrad[:, kcols] = (acc_k[...].astype(BF16).astype(F32) * slope[:, kcols]).astype(BF16)
        for s in range(min(pairs, bits - 1)):

            @pl.when(p == s)
            def _():
                for chain in (0, 1):
                    advance(chain, s)

        return carry

    lax.fori_loop(0, pairs, backward, 0)

    def tokens_back(c, carry):
        r = pl.ds(pl.multiple_of(c * QB, QB), QB)
        dout[r, :] = (
            og_ref[r, :].astype(F32) + dot_nt(hgrad[r, :], w_ref[:, : 4 * width])
        ).astype(BF16)
        return carry

    lax.fori_loop(0, nq, tokens_back, 0)

    def send_rows(c, carry):
        part = dot_nn(scatter_chunk(dest_ref, c * QB, QB), dout[...]).astype(BF16)
        outbox[pl.ds(c * group, group)] = part.reshape(group, cap, width)
        return carry

    lax.fori_loop(0, nq, send_rows, 0)
    start_exchange(n, me, outbox, inbox2, ssem2, rsem2)
    wide = 3 * width // 2
    weight_grad(2, tok_ref, hgrad, width, wide)
    weight_grad(3, tok_ref, hgrad, width + wide, wide)
    inbox2[me] = outbox[me]
    for stage in range(min(pairs, bits - 1), bits):
        advance(0, stage)
        advance(1, stage)
    for stage in range(bits):
        advance(2, stage)
        advance(3, stage)
    finish_exchange(n, me, outbox, inbox2, ssem2, rsem2)
    store = pltpu.make_async_copy(inbox2, ret_ref, lsem.at[0])
    store.start()
    store.wait()


def finish_kernel(scale, home_ref, ret_ref, fi_ref, fo_ref, mi_ref, mo_ref, ev_ref, ni_ref, no_ref, pick):
    rows, width = ev_ref.shape
    gather_matrix(home_ref, pick)
    step = 256
    back = ret_ref[...].reshape(rows, width)
    for c in range(rows // step):
        ev_ref[c * step : (c + 1) * step] = dot_nn(pick[c * step : (c + 1) * step], back).astype(BF16)
    cols = 0
    for ref in fi_ref:
        wide = ref.shape[1]
        ni_ref[:, cols : cols + wide] = DECAY * mi_ref[:, cols : cols + wide] + scale * ref[...]
        cols += wide
    no_ref[...] = DECAY * mo_ref[...] + scale * fo_ref[...]


def finish_entry(scale, home, ret, fa, fb, fc, fo, mi, mo, ev, ni, no, pick):
    finish_kernel(scale, home, ret, (fa, fb, fc), fo, mi, mo, ev, ni, no, pick)


def shards(n, events, home_slot, dest_slot, seq_lens, weights, out_grad, momentum_in, momentum_out):
    rows, width = events.shape
    cap = rows // n
    bits = n.bit_length() - 1
    per = width // n
    fold = max(1, 16 // per)
    tall = per * fold
    home = home_slot.reshape(1, rows)
    dest = dest_slot.reshape(1, rows)
    vm = pl.BlockSpec(memory_space=pltpu.VMEM)
    sm = pl.BlockSpec(memory_space=pltpu.SMEM)
    hbm = pl.BlockSpec(memory_space=pl.ANY)
    dma = pltpu.SemaphoreType.DMA
    wides = (width, width, 3 * width // 2, 3 * width // 2)
    thins = [w // fold for w in wides]
    bufs = [pltpu.VMEM((n * tall, t), BF16) for t in thins]
    for t in thins:
        for stage in range(bits):
            size = (n * tall >> (stage + 1), t)
            bufs.append(pltpu.VMEM(size, BF16))

    def area(r, c, kind=BF16):
        return pltpu.VMEM((r, c), kind)

    boxed = pltpu.VMEM((n, cap, width), BF16)
    ret, *parts = pl.pallas_call(
        functools.partial(step_kernel, n),
        out_shape=[jax.ShapeDtypeStruct((n, cap, width), BF16)]
        + [jax.ShapeDtypeStruct((tall, t), F32) for t in thins],
        in_specs=[sm, vm, vm, vm, hbm, hbm],
        out_specs=[hbm] + [vm] * 4,
        scratch_shapes=[
            area(width, 5 * width),
            area(rows, width),
            boxed,
            boxed,
            boxed,
            area(rows, rows),
            area(rows, width),
            area(rows, width),
            area(rows, 4 * width),
            area(rows, width, F32),
            area(rows, width),
            area(rows, width),
            area(rows, width),
            area(rows, width, F32),
            area(rows, 4 * width),
            area(rows, rows),
            area(rows, rows),
            area(rows, width),
            area(rows, width),
            area(rows, 128, F32),
            area(rows, 128, F32),
            area(n * tall, rows),
            dma((2,)),
            dma((n,)),
            dma((n,)),
            dma((n,)),
            dma((n,)),
            dma((4 * bits,)),
            dma((4 * bits,)),
        ]
        + bufs,
        compiler_params=pltpu.CompilerParams(
            collective_id=0, has_side_effects=True, vmem_limit_bytes=VMEM_LIMIT
        ),
        name="step",
    )(seq_lens, home, dest, events, weights, out_grad)
    f0, f1, f2, f3 = [
        f.reshape(fold, per, f.shape[1]).transpose(1, 0, 2).reshape(per, fold * f.shape[1])
        for f in parts
    ]
    return pl.pallas_call(
        functools.partial(finish_entry, (n * rows) ** (-0.5)),
        out_shape=[
            jax.ShapeDtypeStruct(events.shape, BF16),
            jax.ShapeDtypeStruct(momentum_in.shape, F32),
            jax.ShapeDtypeStruct(momentum_out.shape, F32),
        ],
        in_specs=[vm] * 8,
        out_specs=[vm] * 3,
        scratch_shapes=[pltpu.VMEM((rows, rows), BF16)],
        compiler_params=pltpu.CompilerParams(vmem_limit_bytes=VMEM_LIMIT),
        name="finish",
    )(home, ret, f0, f2, f3, f1, momentum_in, momentum_out)


def solution(mesh):
    n = mesh.shape["dp"]
    row = P("dp", None)
    return jax.shard_map(
        functools.partial(shards, n),
        mesh=mesh,
        in_specs=(row, P("dp"), P("dp"), P("dp"), P(), row, row, row),
        out_specs=(row, row, row),
        check_vma=False,
    )
```

time: 135 us -> 113 us (0.84)
  Pallas kernels: 129 us -> 111 us
  other arithmetic: 2.98 us -> 0 us
  local copies, waits for them, and re-layouts: 2.27 us -> 0 us
    pallas_call x3 -> x2, Pallas kernels: 129 us -> 111 us  [the longest x1 107 us: shards(): pl.pallas_call(functools.partial(step_kernel, n), out_shape=[jax.ShapeDty...]
    add x2 -> x0, other arithmetic: 2.98 us -> none  [the longest x1 1.59 us: shards(): DECAY * momentum_in + grad_scale * sums[:, :4 * width]]
    unnamed x5 -> x0, local copies, waits for them, and re-layouts: 2.27 us -> none
where the time goes in v2:
time: 113 us; the launch traced here: 111 us
  Pallas kernels  111 us (98%)
    pallas_call x1, Pallas kernels, shards(): pl.pallas_call(functools.partial(step_kernel, n), out_shape=[jax.ShapeDty...  107 us
    pallas_call x1, Pallas kernels, shards(): pl.pallas_call(functools.partial(finish_entry, (n * rows) ** (-0.5)), out...  3.65 us

profile of v2, /device:TPU:0, one launch (start us, length us, event | category | flops | bytes accessed | tf_op | source)
XLA Modules:
  0.0 111.3 jit_solution(10514380603753971814)
XLA Ops:
  0.6 107.0 %step.1 = (bf16[32,32,512]{2,1,0:T(8,128)(2,1)}, f32[16,512]{1,0:T(8,128)}, f32[16,512]{1,0:T(8,128)}, f32[16,768]{1,0:T(8,128)}, f32[16,768]{1,0:T(8,128)}) custom-call(s32[2]{0:T(128)} %lens_ref.1, s32[1,1024]{1,0:T(1,128)} %bitcast.2, s32[1,1024]{1,0:T(1,128)} %bitcast.4, bf16[1024,512]{1,0:T(8,128)(2,1)} %ev_ref.1, bf16[512,2560]{1,0:T(8,128)(2,1)} %w_hbm.1, ...), custom_call_target="tpu_custom_call" | custom-call | tf_op jit(solution)/shard_map/step/pallas_call | solution.py:414
  107.7 3.6 %finish.1 = (bf16[1024,512]{1,0:T(8,128)(2,1)}, f32[16,2048]{1,0:T(8,128)}, f32[16,512]{1,0:T(8,128)}) custom-call(s32[1,1024]{1,0:T(1,128)} %bitcast.3, bf16[32,32,512]{2,1,0:T(8,128)(2,1)} %get-tuple-element.8.ret, f32[16,512]{1,0:T(8,128)} %get-tuple-element.9.fa, f32[16,768]{1,0:T(8,128)} %get-tuple-element.10.fb, f32[16,768]{1,0:T(8,128)} %get-tuple-element.11.fc, ...), custom_call_target="tpu_custom_call" | custom-call | tf_op jit(solution)/shard_map/finish/pallas_call | solution.py:461

commit v3 on v1

--- a/solution.py
+++ b/solution.py
@@ -10,12 +10,13 @@
 HEADS = 8
 BLK = 512
 QB = 256
+SECOND = (False, True, False, True, False, False, True, True)
 NORM_EPS = 1e-05
 DECAY = 0.9
 MESH = pl.DeviceIdType.MESH
 F32 = jnp.float32
 BF16 = jnp.bfloat16
-VMEM_LIMIT = 60 * 1024 * 1024
+VMEM_LIMIT = 66 * 1000 * 1000
 
 
 def dot_nn(a, b):
@@ -94,31 +95,6 @@
     return jnp.where(place == slots_ref[...], 1.0, 0.0).astype(BF16)
 
 
-def inbound_kernel(n, home_ref, dest_ref, ev_ref, tok_ref, outbox, inbox, pick, ssem, rsem):
-    me = lax.axis_index("dp")
-    rows, width = ev_ref.shape
-    cap = rows // n
-    barrier = enter_all(n, me)
-    step = 256
-    group = step // cap
-
-    def fill(c, carry):
-        part = dot_nn(scatter_chunk(home_ref, c * step, step), ev_ref[...]).astype(BF16)
-        outbox[pl.ds(c * group, group)] = part.reshape(group, cap, width)
-        return carry
-
-    lax.fori_loop(0, rows // step, fill, 0)
-    pl.semaphore_wait(barrier, n - 1)
-    start_exchange(n, me, outbox, inbox, ssem, rsem)
-    inbox[me] = outbox[me]
-    gather_matrix(dest_ref, pick)
-    finish_exchange(n, me, outbox, inbox, ssem, rsem)
-    for c in range(rows // step):
-        tok_ref[c * step : (c + 1) * step] = dot_nn(
-            pick[c * step : (c + 1) * step], inbox[...].reshape(rows, width)
-        ).astype(BF16)
-
-
 def owner_of(place, lens_ref, none):
     owner = jnp.full(place.shape, none, jnp.int32)
     start = 0
@@ -130,37 +106,81 @@
     return owner
 
 
-def order_matrix(shape, n, per, bits):
-    width = shape[1]
+def order_matrix(height, width, n, per, bits, fold, turn):
+    shape = (height, width)
+    tall = per * fold
     place = lax.broadcasted_iota(jnp.int32, shape, 0)
     column = lax.broadcasted_iota(jnp.int32, shape, 1)
-    slot = place // per
+    slot = place // tall
+    rest = place % tall
     device = jnp.zeros(shape, jnp.int32)
     for rank, bit in enumerate(bits):
         weight = n >> (rank + 1)
         device = device + ((slot // weight) % 2) * (1 << bit)
-    return jnp.where(column == device * per + place % per, 1.0, 0.0).astype(BF16)
-
-
-def layer_kernel(
-    n, lens_ref, dest_ref, tok_ref, w_ref, og_ref,
-    back_ref, ga_ref, gb_ref,
-    slope, gate, qs, ks, vs, att, hgrad, mask, mask_t, mixed, dout, tgrad, acc_k, acc_v, tp,
+    hit = (column == device * per + rest % per) & (rest // per == turn)
+    return jnp.where(hit, 1.0, 0.0).astype(BF16)
+
+
+def step_kernel(
+    n, lens_ref, home_ref, dest_ref, ev_ref, w_hbm, og_hbm,
+    ret_ref, f0_ref, f1_ref, f2_ref, f3_ref, f4_ref, f5_ref, f6_ref, f7_ref,
+    w_ref, og_ref, outbox, inbox, inbox2, pick, tok_ref, dmix,
+    slope, gate, qs, ks, vs, att, hgrad, mask, mask_t, mixed, dout, acc_k, acc_v, tp,
+    lsem, ssem, rsem, ssem2, rsem2, hs, hr, *bufs,
 ):
-    rows, width = tok_ref.shape
+    me = lax.axis_index("dp")
+    rows, width = ev_ref.shape
+    cap = rows // n
     per = width // n
+    fold = max(1, 16 // per)
     nq = rows // QB
     bits = n.bit_length() - 1
+    group = QB // cap
+    barrier = enter_all(n, me)
+    load_w = pltpu.make_async_copy(w_hbm, w_ref, lsem.at[0])
+    load_og = pltpu.make_async_copy(og_hbm, og_ref, lsem.at[1])
+    load_w.start()
+    load_og.start()
+
+    def fill(c, carry):
+        part = dot_nn(scatter_chunk(home_ref, c * QB, QB), ev_ref[...]).astype(BF16)
+        outbox[pl.ds(c * group, group)] = part.reshape(group, cap, width)
+        return carry
+
+    lax.fori_loop(0, nq, fill, 0)
+    pl.semaphore_wait(barrier, n - 1)
+    start_exchange(n, me, outbox, inbox, ssem, rsem)
+    inbox[me] = outbox[me]
+    gather_matrix(dest_ref, pick)
+    load_w.wait()
+    load_og.wait()
+
+    def prepare(c, carry):
+        r = pl.ds(pl.multiple_of(c * QB, QB), QB)
+        low = lax.broadcasted_iota(jnp.int32, (QB, rows), 0) + c * QB
+        high = lax.broadcasted_iota(jnp.int32, (QB, rows), 1)
+        low_col = lax.broadcasted_iota(jnp.int32, (QB, 1), 0) + c * QB
+        high_row = lax.broadcasted_iota(jnp.int32, (1, rows), 1)
+        q_own = owner_of(low_col, lens_ref, -1)
+        k_own = owner_of(high_row, lens_ref, -2)
+        mask[r, :] = jnp.where((q_own == k_own) & (high <= low), 1.0, 0.0).astype(BF16)
+        mask_t[r, :] = jnp.where((q_own == k_own) & (low <= high), 1.0, 0.0).astype(BF16)
+        dmix[r, :] = dot_nt(og_ref[r, :], w_ref[:, 4 * width :]).astype(BF16)
+        return carry
+
+    lax.fori_loop(0, nq, prepare, 0)
+    finish_exchange(n, me, outbox, inbox, ssem, rsem)
 
     def project(c, carry):
         r = pl.ds(pl.multiple_of(c * QB, QB), QB)
-        x = tok_ref[r, :]
+        x = dot_nn(pick[r, :], inbox[...].reshape(rows, width)).astype(BF16)
+        tok_ref[r, :] = x
         for g in range(4):
             cols = slice(g * width, (g + 1) * width)
             u = dot_nn(x, w_ref[:, cols]) * 0.5
             t = jnp.tanh(u)
             a = u * t + u
-            slope[r, cols] = 0.5 * ((1.0 + a) + t * (1.0 - a))
+            slope[r, cols] = (0.5 * ((1.0 + a) + t * (1.0 - a))).astype(BF16)
             if g == 0:
                 gate[r, :] = a
             elif g == 1:
@@ -169,14 +189,6 @@
                 qs[r, :] = (a.astype(BF16).astype(F32) * (0.5 * (width // HEADS) ** -0.5)).astype(BF16)
             else:
                 ks[r, :] = a.astype(BF16)
-        low = lax.broadcasted_iota(jnp.int32, (QB, rows), 0) + c * QB
-        high = lax.broadcasted_iota(jnp.int32, (QB, rows), 1)
-        low_col = lax.broadcasted_iota(jnp.int32, (QB, 1), 0) + c * QB
-        high_row = lax.broadcasted_iota(jnp.int32, (1, rows), 1)
-        q_own = owner_of(low_col, lens_ref, -1)
-        k_own = owner_of(high_row, lens_ref, -2)
-        mask[r, :] = jnp.where((q_own == k_own) & (high <= low), 1.0, 0.0).astype(BF16)
-        mask_t[r, :] = jnp.where((q_own == k_own) & (low <= high), 1.0, 0.0).astype(BF16)
         return carry
 
     lax.fori_loop(0, nq, project, 0)
@@ -212,15 +224,92 @@
         unit = centred * inv
         g = gate[r, :]
         mixed[r, :] = (unit * g).astype(BF16)
-        dmix = dot_nt(og_ref[r, :], w_ref[:, 4 * width :])
-        hgrad[r, :width] = (dmix * unit * slope[r, :width]).astype(BF16)
-        dn = dmix * g
+        dm = dmix[r, :].astype(F32)
+        hgrad[r, :width] = (dm * unit * slope[r, :width]).astype(BF16)
+        dn = dm * g
         mean_a = jnp.mean(dn, axis=1, keepdims=True)
         mean_b = jnp.mean(dn * unit, axis=1, keepdims=True)
         dout[r, :] = (inv * (dn - mean_a - unit * mean_b)).astype(BF16)
         return carry
 
     lax.fori_loop(0, nq, norm, 0)
+
+    pairs = width // pair_width
+    sources = bufs[:8]
+    hops = bufs[8:]
+    sums = (f0_ref, f1_ref, f2_ref, f3_ref, f4_ref, f5_ref, f6_ref, f7_ref)
+
+    def hop(chain, stage):
+        bit = chain_bits(bits, SECOND[chain])[stage]
+        mine = (me // (1 << bit)) % 2
+        peer = me + (1 - 2 * mine) * (1 << bit)
+        cur = sources[chain] if stage == 0 else hops[chain * bits + stage - 1]
+        got = hops[chain * bits + stage]
+        half = cur.shape[0] // 2
+        copy = pltpu.make_async_remote_copy(
+            src_ref=cur.at[pl.ds((1 - mine) * half, half)],
+            dst_ref=got,
+            send_sem=hs.at[chain * bits + stage],
+            recv_sem=hr.at[chain * bits + stage],
+            device_id=(peer,),
+            device_id_type=MESH,
+        )
+        return copy, cur.at[pl.ds(mine * half, half)], got
+
+    def advance(chain, stage):
+        copy, kept, got = hop(chain, stage)
+        copy.wait()
+        total = kept[...].astype(F32) + got[...].astype(F32)
+        if stage == bits - 1:
+            sums[chain][...] = total
+        else:
+            got[...] = total.astype(BF16)
+            hop(chain, stage + 1)[0].start()
+
+    height = n * per * fold
+    roomy = fold == 1 and 2 * height <= rows
+
+    def turned(left, second, turn, out):
+        order = order_matrix(height, width, n, per, chain_bits(bits, second), fold, turn)
+        out[...] = dot_nt(order, left[...]).astype(BF16)
+        return out
+
+    if roomy:
+        kept_rows = [
+            turned(tok_ref, second, 0, pick.at[pl.ds(int(second) * height, height)])
+            for second in (False, True)
+        ]
+
+    def weight_grad(chain, left, right, base, wide):
+        thin = wide // fold
+        for turn in range(fold):
+            if roomy and left is tok_ref:
+                lhs = kept_rows[int(SECOND[chain])]
+            else:
+                lhs = turned(left, SECOND[chain], turn, tp)
+            step = 256 if thin % 256 == 0 else thin
+            for j in range(thin // step):
+                start = base + turn * thin + j * step
+                part = dot_nn(lhs[...], right[:, start : start + step])
+                cols = slice(j * step, (j + 1) * step)
+                if turn == 0:
+                    sources[chain][:, cols] = part.astype(BF16)
+                else:
+                    sources[chain][:, cols] += part.astype(BF16)
+        hop(chain, 0)[0].start()
+
+    def part_grads(second_half):
+        for g in range(3):
+            base = (g + 1) * width + second_half * (width // 2)
+            weight_grad(2 + 3 * second_half + g, tok_ref, hgrad, base, width // 2)
+
+    def advance_all(chains, stage):
+        if stage < bits:
+            for chain in chains:
+                advance(chain, stage)
+
+    weight_grad(0, tok_ref, hgrad, 0, width)
+    weight_grad(1, mixed, og_ref, 0, width)
 
     def backward(p, carry):
         off = pl.multiple_of(p * pair_width, pair_width)
@@ -259,6 +348,328 @@
         kcols = pl.ds(3 * width + off, pair_width)
         hgrad[:, vcols] = (acc_v[...].astype(BF16).astype(F32) * slope[:, vcols]).astype(BF16)
         hgrad[:, kcols] = (acc_k[...].astype(BF16).astype(F32) * slope[:, kcols]).astype(BF16)
+        for s in range(pairs):
+
+            @pl.when(p == s)
+            def _():
+                advance_all((0, 1), s)
+                if s == pairs // 2 - 1:
+                    part_grads(0)
+                elif s >= pairs // 2:
+                    advance_all((2, 3, 4), s - pairs // 2)
+
+        return carry
+
+    lax.fori_loop(0, pairs, backward, 0)
+    part_grads(1)
+    early = pairs - pairs // 2
+    for stage in range(pairs, bits):
+        advance_all((0, 1), stage)
+    advance_all((2, 3, 4), early)
+
+    def tokens_back(c, carry):
+        r = pl.ds(pl.multiple_of(c * QB, QB), QB)
+        dout[r, :] = (
+            og_ref[r, :].astype(F32) + dot_nt(hgrad[r, :], w_ref[:, : 4 * width])
+        ).astype(BF16)
+        return carry
+
+    lax.fori_loop(0, nq, tokens_back, 0)
+    advance_all((2, 3, 4), early + 1)
+    advance_all((5, 6, 7), 0)
+
+    def send_rows(c, carry):
+        part = dot_nn(scatter_chunk(dest_ref, c * QB, QB), dout[...]).astype(BF16)
+        outbox[pl.ds(c * group, group)] = part.reshape(group, cap, width)
+        return carry
+
+    lax.fori_loop(0, nq, send_rows, 0)
+
+    def some(low, high):
+        def go(i, carry):
+            exchange(n, me, outbox, inbox2, ssem2, rsem2, i).start()
+            return carry
+
+        lax.fori_loop(low, high, go, 0)
+
+    some(n // 2, 7 * n // 8)
+    inbox2[me] = outbox[me]
+    for stage in range(early + 2, bits):
+        advance_all((2, 3, 4), stage)
+    advance_all((5, 6, 7), 1)
+    some(7 * n // 8, n)
+    some(1, n // 8)
+    advance_all((5, 6, 7), 2)
+    some(n // 8, n // 2)
+    for stage in range(3, bits):
+        advance_all((5, 6, 7), stage)
+    finish_exchange(n, me, outbox, inbox2, ssem2, rsem2)
+    store = pltpu.make_async_copy(inbox2, ret_ref, lsem.at[0])
+    store.start()
+    store.wait()
+
+
+def finish_kernel(scale, home_ref, ret_ref, fi_ref, fo_ref, mi_ref, mo_ref, ev_ref, ni_ref, no_ref, pick):
+    rows, width = ev_ref.shape
+    gather_matrix(home_ref, pick)
+    step = 256
+    back = ret_ref[...].reshape(rows, width)
+    for c in range(rows // step):
+        ev_ref[c * step : (c + 1) * step] = dot_nn(pick[c * step : (c + 1) * step], back).astype(BF16)
+    cols = 0
+    for ref in fi_ref:
+        wide = ref.shape[1]
+        ni_ref[:, cols : cols + wide] = DECAY * mi_ref[:, cols : cols + wide] + scale * ref[...]
+        cols += wide
+    no_ref[...] = DECAY * mo_ref[...] + scale * fo_ref[...]
+
+
+def finish_entry(scale, home, ret, f0, f1, f2, f3, f4, f5, f6, fo, mi, mo, ev, ni, no, pick):
+    fi = (f0, f1, f2, f3, f4, f5, f6)
+    finish_kernel(scale, home, ret, fi, fo, mi, mo, ev, ni, no, pick)
+
+
+def shards(n, events, home_slot, dest_slot, seq_lens, weights, out_grad, momentum_in, momentum_out):
+    rows, width = events.shape
+    cap = rows // n
+    bits = n.bit_length() - 1
+    per = width // n
+    fold = max(1, 16 // per)
+    tall = per * fold
+    home = home_slot.reshape(1, rows)
+    dest = dest_slot.reshape(1, rows)
+    vm = pl.BlockSpec(memory_space=pltpu.VMEM)
+    sm = pl.BlockSpec(memory_space=pltpu.SMEM)
+    hbm = pl.BlockSpec(memory_space=pl.ANY)
+    dma = pltpu.SemaphoreType.DMA
+    wides = (width, width) + (width // 2,) * 6
+    thins = [w // fold for w in wides]
+    bufs = [pltpu.VMEM((n * tall, t), BF16) for t in thins]
+    for t in thins:
+        for stage in range(bits):
+            size = (n * tall >> (stage + 1), t)
+            bufs.append(pltpu.VMEM(size, BF16))
+
+    def area(r, c, kind=BF16):
+        return pltpu.VMEM((r, c), kind)
+
+    boxed = pltpu.VMEM((n, cap, width), BF16)
+    ret, *parts = pl.pallas_call(
+        functools.partial(step_kernel, n),
+        out_shape=[jax.ShapeDtypeStruct((n, cap, width), BF16)]
+        + [jax.ShapeDtypeStruct((tall, t), F32) for t in thins],
+        in_specs=[sm, vm, vm, vm, hbm, hbm],
+        out_specs=[hbm] + [vm] * 8,
+        scratch_shapes=[
+            area(width, 5 * width),
+            area(rows, width),
+            boxed,
+            boxed,
+            boxed,
+            area(rows, rows),
+            area(rows, width),
+            area(rows, width),
+            area(rows, 4 * width),
+            area(rows, width, F32),
+            area(rows, width),
+            area(rows, width),
+            area(rows, width),
+            area(rows, width, F32),
+            area(rows, 4 * width),
+            area(rows, rows),
+            area(rows, rows),
+            area(rows, width),
+            area(rows, width),
+            area(rows, 128, F32),
+            area(rows, 128, F32),
+            area(n * tall, rows),
+            dma((2,)),
+            dma((n,)),
+            dma((n,)),
+            dma((n,)),
+            dma((n,)),
+            dma((8 * bits,)),
+            dma((8 * bits,)),
+        ]
+        + bufs,
+        compiler_params=pltpu.CompilerParams(
+            collective_id=0, has_side_effects=True, vmem_limit_bytes=VMEM_LIMIT
+        ),
+        name="step",
+    )(seq_lens, home, dest, events, weights, out_grad)
+    gate_sum, out_sum, va, qa, ka, vb, qb, kb = [
+        f.reshape(fold, per, f.shape[1]).transpose(1, 0, 2).reshape(per, fold * f.shape[1])
+        for f in parts
+    ]
+    return pl.pallas_call(
+        functools.partial(finish_entry, (n * rows) ** (-0.5)),
+        out_shape=[
+            jax.ShapeDtypeStruct(events.shape, BF16),
+            jax.ShapeDtypeStruct(momentum_in.shape, F32),
+            jax.ShapeDtypeStruct(momentum_out.shape, F32),
+        ],
+        in_specs=[vm] * 12,
+        out_specs=[vm] * 3,
+        scratch_shapes=[pltpu.VMEM((rows, rows), BF16)],
+        compiler_params=pltpu.CompilerParams(vmem_limit_bytes=VMEM_LIMIT),
+        name="finish",
+    )(home, ret, gate_sum, va, vb, qa, qb, ka, kb, out_sum, momentum_in, momentum_out)
+
+
+def inbound_kernel(n, home_ref, dest_ref, ev_ref, tok_ref, outbox, inbox, pick, ssem, rsem):
+    me = lax.axis_index("dp")
+    rows, width = ev_ref.shape
+    cap = rows // n
+    barrier = enter_all(n, me)
+    step = 256
+    group = step // cap
+
+    def fill(c, carry):
+        part = dot_nn(scatter_chunk(home_ref, c * step, step), ev_ref[...]).astype(BF16)
+        outbox[pl.ds(c * group, group)] = part.reshape(group, cap, width)
+        return carry
+
+    lax.fori_loop(0, rows // step, fill, 0)
+    pl.semaphore_wait(barrier, n - 1)
+    start_exchange(n, me, outbox, inbox, ssem, rsem)
+    inbox[me] = outbox[me]
+    gather_matrix(dest_ref, pick)
+    finish_exchange(n, me, outbox, inbox, ssem, rsem)
+    for c in range(rows // step):
+        tok_ref[c * step : (c + 1) * step] = dot_nn(
+            pick[c * step : (c + 1) * step], inbox[...].reshape(rows, width)
+        ).astype(BF16)
+
+
+def order_plain(shape, n, per, bits):
+    width = shape[1]
+    place = lax.broadcasted_iota(jnp.int32, shape, 0)
+    column = lax.broadcasted_iota(jnp.int32, shape, 1)
+    slot = place // per
+    device = jnp.zeros(shape, jnp.int32)
+    for rank, bit in enumerate(bits):
+        weight = n >> (rank + 1)
+        device = device + ((slot // weight) % 2) * (1 << bit)
+    return jnp.where(column == device * per + place % per, 1.0, 0.0).astype(BF16)
+
+
+def layer_kernel(
+    n, lens_ref, dest_ref, tok_ref, w_ref, og_ref,
+    back_ref, ga_ref, gb_ref,
+    slope, gate, qs, ks, vs, att, hgrad, mask, mask_t, mixed, dout, tgrad, acc_k, acc_v, tp,
+):
+    rows, width = tok_ref.shape
+    per = width // n
+    nq = rows // QB
+    bits = n.bit_length() - 1
+
+    def project(c, carry):
+        r = pl.ds(pl.multiple_of(c * QB, QB), QB)
+        x = tok_ref[r, :]
+        for g in range(4):
+            cols = slice(g * width, (g + 1) * width)
+            u = dot_nn(x, w_ref[:, cols]) * 0.5
+            t = jnp.tanh(u)
+            a = u * t + u
+            slope[r, cols] = 0.5 * ((1.0 + a) + t * (1.0 - a))
+            if g == 0:
+                gate[r, :] = a
+            elif g == 1:
+                vs[r, :] = a.astype(BF16)
+            elif g == 2:
+                qs[r, :] = (a.astype(BF16).astype(F32) * (0.5 * (width // HEADS) ** -0.5)).astype(BF16)
+            else:
+                ks[r, :] = a.astype(BF16)
+        low = lax.broadcasted_iota(jnp.int32, (QB, rows), 0) + c * QB
+        high = lax.broadcasted_iota(jnp.int32, (QB, rows), 1)
+        low_col = lax.broadcasted_iota(jnp.int32, (QB, 1), 0) + c * QB
+        high_row = lax.broadcasted_iota(jnp.int32, (1, rows), 1)
+        q_own = owner_of(low_col, lens_ref, -1)
+        k_own = owner_of(high_row, lens_ref, -2)
+        mask[r, :] = jnp.where((q_own == k_own) & (high <= low), 1.0, 0.0).astype(BF16)
+        mask_t[r, :] = jnp.where((q_own == k_own) & (low <= high), 1.0, 0.0).astype(BF16)
+        return carry
+
+    lax.fori_loop(0, nq, project, 0)
+
+    pair_width = 128
+    head = width // HEADS
+    lane = lax.broadcasted_iota(jnp.int32, (1, pair_width), 1) // head
+    picks = [jnp.where(lane == h, 1.0, 0.0).astype(BF16) for h in range(pair_width // head)]
+
+    def forward(p, carry):
+        cols = pl.ds(pl.multiple_of(p * pair_width, pair_width), pair_width)
+        for c in range(nq):
+            top = (c + 1) * QB
+            r = slice(c * QB, top)
+            out = None
+            for sel in picks:
+                u = dot_nt(qs[r, cols] * sel, ks[:top, cols])
+                t = jnp.tanh(u)
+                a = (u * t + u).astype(BF16) * mask[r, :top]
+                o = dot_nn(a, vs[:top, cols] * sel)
+                out = o if out is None else out + o
+            att[r, cols] = out
+        return carry
+
+    lax.fori_loop(0, width // pair_width, forward, 0)
+
+    def norm(c, carry):
+        r = pl.ds(pl.multiple_of(c * QB, QB), QB)
+        x = att[r, :]
+        centred = x - jnp.mean(x, axis=1, keepdims=True)
+        spread = jnp.mean(centred * centred, axis=1, keepdims=True)
+        inv = lax.rsqrt(spread + NORM_EPS)
+        unit = centred * inv
+        g = gate[r, :]
+        mixed[r, :] = (unit * g).astype(BF16)
+        dmix = dot_nt(og_ref[r, :], w_ref[:, 4 * width :])
+        hgrad[r, :width] = (dmix * unit * slope[r, :width]).astype(BF16)
+        dn = dmix * g
+        mean_a = jnp.mean(dn, axis=1, keepdims=True)
+        mean_b = jnp.mean(dn * unit, axis=1, keepdims=True)
+        dout[r, :] = (inv * (dn - mean_a - unit * mean_b)).astype(BF16)
+        return carry
+
+    lax.fori_loop(0, nq, norm, 0)
+
+    def backward(p, carry):
+        off = pl.multiple_of(p * pair_width, pair_width)
+        cols = pl.ds(off, pair_width)
+        for c in range(nq):
+            top = (c + 1) * QB
+            r = slice(c * QB, top)
+            dq = None
+            for sel in picks:
+                qm = qs[r, cols] * sel
+                dm = dout[r, cols] * sel
+                u = dot_nt(ks[:top, cols], qm)
+                t = jnp.tanh(u)
+                a = u * t + u
+                m = mask_t[:top, r]
+                d = dot_nt(vs[:top, cols], dm)
+                ds = (d * ((1.0 + a) + t * (1.0 - a))).astype(BF16) * m
+                pb = a.astype(BF16) * m
+                dv = dot_nn(pb, dm)
+                dk = dot_nn(ds, qm)
+                part = dot_tn(ds, ks[:top, cols] * sel)
+                dq = part if dq is None else dq + part
+                if c > 0:
+                    acc_v[: c * QB, :] += dv[: c * QB]
+                    acc_k[: c * QB, :] += dk[: c * QB]
+                if sel is picks[0]:
+                    acc_v[c * QB : top, :] = dv[c * QB :]
+                    acc_k[c * QB : top, :] = dk[c * QB :]
+                else:
+                    acc_v[c * QB : top, :] += dv[c * QB :]
+                    acc_k[c * QB : top, :] += dk[c * QB :]
+            qcols = pl.ds(2 * width + off, pair_width)
+            dq = (dq * (0.5 * head**-0.5)).astype(BF16).astype(F32)
+            hgrad[r, qcols] = (dq * slope[r, qcols]).astype(BF16)
+        vcols = pl.ds(width + off, pair_width)
+        kcols = pl.ds(3 * width + off, pair_width)
+        hgrad[:, vcols] = (acc_v[...].astype(BF16).astype(F32) * slope[:, vcols]).astype(BF16)
+        hgrad[:, kcols] = (acc_k[...].astype(BF16).astype(F32) * slope[:, kcols]).astype(BF16)
         return carry
 
     lax.fori_loop(0, width // pair_width, backward, 0)
@@ -284,7 +695,7 @@
     half = ga_ref.shape[1]
     step = 256
     for ref, base, second in ((ga_ref, 0, False), (gb_ref, half, True)):
-        order = order_matrix((width, width), n, per, chain_bits(bits, second))
+        order = order_plain((width, width), n, per, chain_bits(bits, second))
         tp[...] = dot_nt(order, tok_ref[...]).astype(BF16)
 
         def columns(j, carry, ref=ref, base=base):
@@ -351,7 +762,7 @@
         ).astype(BF16)
 
 
-def shards(n, events, home_slot, dest_slot, seq_lens, weights, out_grad, momentum_in, momentum_out):
+def shards_small(n, events, home_slot, dest_slot, seq_lens, weights, out_grad, momentum_in, momentum_out):
     rows, width = events.shape
     cap = rows // n
     bits = n.bit_length() - 1
@@ -453,7 +864,7 @@
     n = mesh.shape["dp"]
     row = P("dp", None)
     return jax.shard_map(
-        functools.partial(shards, n),
+        functools.partial(shards if BLK // n >= 16 else shards_small, n),
         mesh=mesh,
         in_specs=(row, P("dp"), P("dp"), P("dp"), P(), row, row, row),
         out_specs=(row, row, row),

time: 135 us -> 114 us (0.84)
  Pallas kernels: 129 us -> 113 us
  other arithmetic: 2.98 us -> 0 us
  local copies, waits for them, and re-layouts: 2.27 us -> 0 us
    pallas_call x3 -> x2, Pallas kernels: 129 us -> 113 us  [the longest x1 109 us: shards(): pl.pallas_call(functools.partial(step_kernel, n), out_shape=[jax.ShapeDty...]
    add x2 -> x0, other arithmetic: 2.98 us -> none  [the longest x1 1.59 us: shards(): DECAY * momentum_in + grad_scale * sums[:, :4 * width]]
    unnamed x5 -> x0, local copies, waits for them, and re-layouts: 2.27 us -> none
where the time goes in v3:
time: 114 us
  Pallas kernels  113 us (99%)
    pallas_call x1, Pallas kernels, shards(): pl.pallas_call(functools.partial(step_kernel, n), out_shape=[jax.ShapeDty...  109 us
    pallas_call x1, Pallas kernels, shards(): pl.pallas_call(functools.partial(finish_entry, (n * rows) ** (-0.5)), out...  3.69 us

profile of v3, /device:TPU:0, one launch (start us, length us, event | category | flops | bytes accessed | tf_op | source)
XLA Modules:
  0.0 113.8 jit_solution(5009528114326516008)
XLA Ops:
  0.6 109.5 %step.1 = (bf16[32,32,512]{2,1,0:T(8,128)(2,1)}, f32[16,512]{1,0:T(8,128)}, f32[16,512]{1,0:T(8,128)}, f32[16,256]{1,0:T(8,128)}, f32[16,256]{1,0:T(8,128)}, /*i...) custom-call(s32[2]{0:T(128)} %lens_ref.1, s32[1,1024]{1,0:T(1,128)} %bitcast.2, ...), custom_call_target="tpu_custom_call" | custom-call | tf_op jit(solution)/shard_map/step/pallas_call | solution.py:457
  110.1 3.7 %finish.1 = (bf16[1024,512]{1,0:T(8,128)(2,1)}, f32[16,2048]{1,0:T(8,128)}, f32[16,512]{1,0:T(8,128)}) custom-call(s32[1,1024]{1,0:T(1,128)} %bitcast.3, bf16[32,32,512]{2,1,0:T(8,128)(2,1)} %get-tuple-element.12.ret, f32[16,512]{1,0:T(8,128)} %get-tuple-element.13.f0, f32[16,256]{1,0:T(8,128)} %get-tuple-element.14.f1, f32[16,256]{1,0:T(8,128)} %get-tuple-element.15.f2, ...), custom_call_target="tpu_custom_call" | custom-call | tf_op jit(solution)/shard_map/finish/pallas_call | solution.py:504
